TPU v7x, 32 devices: a whole 2x2x4 slice. The times are simulated.
32 devices in a mesh: station: 8 (over y, x, core), tm: 4 (over z).
Axes of the slice: x: 2, y: 2, z: 4, core: 2. Of those that a mesh axis runs over, the one named last changes fastest.
Arguments:
- samples: bfloat16 [64, 256, 2048], P('tm', 'station'), may hold values from -6 to 6
- history: bfloat16 [15, 256, 2048], P(None, 'station'), may hold values from -6 to 6
- taps: float32 [16, 2048], replicated, may hold values from -0.03125 to 0.03125
Outputs:
- visibility: float32 [1024, 2, 256, 256], P(('station', 'tm'))
- beam_power: float32 [64, 1024], P('tm', 'station')
All inputs are finite; a program needn't handle non-finite values.
Results may differ from a plain program's by a relative error of at most 0.0095.
Values may be sent and summed in bfloat16 or wider, within the bound.
A program may use at most 128 MiB of HBM per device.

v0:
```python
import math

import jax
import jax.numpy as jnp
from jax import lax
from jax.sharding import PartitionSpec as P


def passed_along(block, axis, distance):
    devices = range(lax.axis_size(axis))
    route = [(i - distance, i) for i in devices if i - distance in devices]
    return lax.ppermute(block, axis, route)


def dft_parts(frame_len, channels):
    sample_index = jnp.arange(frame_len, dtype=jnp.int32)
    channel_index = jnp.arange(channels, dtype=jnp.int32)
    phases = sample_index[:, None] * channel_index[None, :] % frame_len
    angles = phases.astype(jnp.float32) * (2.0 * math.pi / frame_len)
    return (jnp.cos(angles).astype(jnp.bfloat16), (-jnp.sin(angles)).astype(jnp.bfloat16))


def filter_frames(extended, taps, frames_out):
    span_taps = taps.shape[0]
    running = jnp.zeros((frames_out,) + extended.shape[1:], jnp.float32)
    for tap_index in range(span_taps):
        offset = span_taps - 1 - tap_index
        running = running + taps[tap_index][None, None, :] * extended[
            offset : offset + frames_out
        ].astype(jnp.float32)
    return jnp.swapaxes(running, 0, 1).astype(jnp.bfloat16)


def power_of(grouped):
    values = grouped.astype(jnp.float32)
    return jnp.sum(values * values, axis=(-3, -2)) * (1.0 / grouped.shape[-3])


def flat_pair(piece):
    chan_count, input_count, pair_count, frame_count = piece.shape
    flat = piece.reshape(chan_count, input_count, pair_count * frame_count)
    rotated = jnp.concatenate([-piece[:, :, 1:2], piece[:, :, 0:1]], axis=2)
    return (flat, rotated.reshape(chan_count, input_count, pair_count * frame_count))


def correlate(piece, norm_scale):
    flat, rotated = flat_pair(piece)
    real_part = (
        jnp.einsum("cak,cbk->cab", flat, flat, preferred_element_type=jnp.float32) * norm_scale
    )
    imag_part = (
        jnp.einsum("cak,cbk->cab", rotated, flat, preferred_element_type=jnp.float32) * norm_scale
    )
    return (real_part, imag_part)


def body(samples, history, taps):
    frames_dev = samples.shape[0]
    frame_len = samples.shape[2]
    span_taps = taps.shape[0]
    cos_part, sin_part = dft_parts(frame_len, frame_len // 2)
    tail_block = samples[frames_dev - (span_taps - 1) :]
    prior_frames = passed_along(tail_block, "tm", 1)
    prior_frames = jnp.where(lax.axis_index("tm") == 0, history, prior_frames)
    extended = jnp.concatenate([prior_frames, samples], axis=0)
    weighted = filter_frames(extended, taps, frames_dev)
    real_spec = jnp.einsum("nc,atn->cat", cos_part, weighted, preferred_element_type=jnp.float32)
    imag_spec = jnp.einsum("nc,atn->cat", sin_part, weighted, preferred_element_type=jnp.float32)
    spectra = jnp.stack([real_spec, imag_spec], axis=2).astype(jnp.bfloat16)
    time_groups = lax.axis_size("tm")
    norm_scale = 1.0 / (frames_dev * time_groups)
    gathered = lax.all_to_all(
        lax.all_to_all(spectra[None], "station", split_axis=1, concat_axis=2, tiled=True),
        "tm",
        split_axis=1,
        concat_axis=0,
        tiled=True,
    )
    own_channels = gathered.shape[1]
    inputs = gathered.shape[2]
    power_own = power_of(gathered)
    power_back = lax.all_to_all(power_own, "tm", split_axis=0, concat_axis=1, tiled=True)
    power_rows = jnp.transpose(power_back[0])

    def accumulate(block_index, running):
        time_piece = lax.dynamic_index_in_dim(gathered, block_index, 0, keepdims=False)
        real_part, imag_part = correlate(time_piece, norm_scale)
        partial_value = jnp.stack([real_part, imag_part], axis=1).astype(jnp.bfloat16)
        partial_value = lax.optimization_barrier(partial_value)
        return running + partial_value.astype(jnp.float32)

    initial_sum = jnp.zeros((own_channels, 2, inputs, inputs), jnp.float32)
    visibility = lax.fori_loop(0, time_groups, accumulate, initial_sum)
    return (visibility, power_rows)


def solution(mesh):
    return jax.shard_map(
        body,
        mesh=mesh,
        in_specs=(P("tm", "station", None), P(None, "station", None), P()),
        out_specs=(P(("station", "tm"), None, None, None), P("tm", "station")),
        check_vma=False,
    )
```

profile of v0, /device:TPU:1, one launch (start us, length us, event | category | flops | bytes accessed | tf_op | source)
XLA Modules:
  0.0 370.1 jit_solution(146463902237839219)
XLA Ops:
  0.6 0.0 copy-start
  0.6 3.2 slice.112
  3.8 5.3 %collective-permute-start = (bf16[15,32,2048]{2,1,0:T(8,128)(2,1)}, bf16[15,32,2048]{2,1,0:T(8,128)(2,1)}, u32[]{:S(2)}, u32[]{:S(2)}) collective-permute-start(bf16[15,32,2048]{2,1,0:T(8,128)(2,1)} %slice.112), channel_id=1, source_target_pairs={{0,1},{1,2},{2,3},{4,5},{5,6},{6,7},{8,9},{9,10},{10,11},{12,13},{... | collective-permute-start | bytes 5898248 | tf_op jit(solution)/shard_map/ppermute | solution.py:12
  9.2 1.6 fusion.60
  10.8 38.9 %collective-permute-done = bf16[15,32,2048]{2,1,0:T(8,128)(2,1)} collective-permute-done((bf16[15,32,2048]{2,1,0:T(8,128)(2,1)}, bf16[15,32,2048]{2,1,0:T(8,128)(2,1)}, u32[]{:S(2)}, u32[]{:S(2)}) %collective-permute-start) | collective-permute-done | bytes 1966112 | tf_op jit(solution)/shard_map/ppermute | solution.py:12
  49.6 1.8 broadcast_select_fusion
  51.4 0.0 copy-done
  51.4 9.5 %add_convert_fusion = bf16[16,32,2048]{2,1,0:T(8,128)(2,1)S(1)} fusion(bf16[16,32,2048]{2,1,0:T(8,128)(2,1)S(1)} %copy-done, bf16[15,32,2048]{2,1,0:T(8,128)(2,1)S(1)} %broadcast_select_fusion, f32[2048]{0:T(1024)S(1)} %bitcast.116, f32[2048]{0:T(1024)S(1)} %bitcast.117, f32[2048]{0:T(1024)S(1)} %bitcast.103, f32[2048]{0:T(1024)S(1)} %bitcast.104, ...), kind=kLoop, calls=%fused_computation.53 | loop fusion | flops 66060288 | bytes 6291456 | tf_op jit(solution)/shard_map/convert_element_type | solution.py:31
  60.9 31.8 %fusion.42 = bf16[1,1024,32,1,16]{1,2,4,3,0:T(8,128)(2,1)S(1)} fusion(bf16[16,32,2048]{2,1,0:T(8,128)(2,1)S(1)} %add_convert_fusion), kind=kOutput, calls=%fused_computation.75 | convolution fusion | flops 2179465216 | bytes 3145728 | tf_op jit(solution)/shard_map/nc,atn->cat/dot_general | solution.py:67
  92.7 32.5 %fusion.47 = bf16[1,1024,32,1,16]{1,2,4,3,0:T(8,128)(2,1)S(1)} fusion(bf16[16,32,2048]{2,1,0:T(8,128)(2,1)S(1)} %add_convert_fusion), kind=kOutput, calls=%fused_computation.76 | convolution fusion | flops 2181562368 | bytes 3145728 | tf_op jit(solution)/shard_map/nc,atn->cat/dot_general | solution.py:68
  125.2 0.2 pad_maximum_fusion.3
  125.4 12.1 %copy.33 = bf16[1,1024,32,2,16]{2,4,3,0,1:T(8,128)(2,1)} copy(bf16[1,1024,32,2,16]{1,2,4,3,0:T(8,128)(2,1)S(1)} %pad_maximum_fusion.3) | data formatting | bytes 4194304 | tf_op jit(solution)/shard_map/stack | solution.py:69
  137.4 10.1 %reshape.82 = bf16[8,2,65536]{2,1,0:T(2,128)(2,1)S(1)} reshape(bf16[1024,1,2,16,32]{4,3,2,1,0:T(8,128)(2,1)} %bitcast.96) | data formatting | bytes 4194304
  147.6 30.4 %all_to_all.39 = bf16[8,2,65536]{2,1,0:T(2,128)(2,1)} all-to-all(bf16[8,2,65536]{2,1,0:T(2,128)(2,1)S(1)} %reshape.82), channel_id=1, replica_groups=mesh['station'=8,'tm'=4] {'station'}, dimensions={0} | all-to-all | bytes 4194304 | tf_op jit(solution)/shard_map/all_to_all | solution.py:73
  178.0 8.6 %reshape.83 = bf16[1024,1,2,16,32]{4,3,2,1,0:T(8,128)(2,1)} reshape(bf16[8,2,65536]{2,1,0:T(2,128)(2,1)} %all_to_all.39) | data formatting | bytes 4194304
  186.6 9.3 %copy.42 = bf16[1,8,128,32,2,16]{2,1,5,4,3,0:T(8,128)(2,1)S(1)} copy(bf16[1,8,128,32,2,16]{3,5,4,2,1,0:T(8,128)(2,1)} %bitcast.97) | data formatting | bytes 4194304 | tf_op jit(solution)/shard_map/all_to_all | solution.py:73
  195.9 1.7 copy.35
  197.6 4.9 %copy.36 = bf16[1,128,256,2,16]{2,4,3,0,1:T(8,128)(2,1)} copy(bf16[1,128,256,2,16]{1,4,3,2,0:T(8,128)(2,1)} %bitcast.99) | data formatting | bytes 4194304 | tf_op jit(solution)/shard_map/all_to_all | solution.py:73
  202.5 5.5 %all-to-all-start.1 = ((bf16[1,128,256,2,16]{2,4,3,0,1:T(8,128)(2,1)}), bf16[1,128,256,2,16]{2,4,3,0,1:T(8,128)(2,1)S(1)}, u32[]{:S(2)}, u32[]{:S(2)}) async-start(bf16[1,128,256,2,16]{2,4,3,0,1:T(8,128)(2,1)} %copy.36), calls=%async_computation.1 | async-start | bytes 4194304 | tf_op jit(solution)/shard_map/all_to_all | solution.py:72
  208.0 47.7 %all-to-all-done.1 = bf16[1,128,256,2,16]{2,4,3,0,1:T(8,128)(2,1)S(1)} async-done(((bf16[1,128,256,2,16]{2,4,3,0,1:T(8,128)(2,1)}), bf16[1,128,256,2,16]{2,4,3,0,1:T(8,128)(2,1)S(1)}, u32[]{:S(2)}, u32[]{:S(2)}) %all-to-all-start.1) | async-done | bytes 2097184 | tf_op jit(solution)/shard_map/all_to_all | solution.py:72
  255.7 0.5 multiply_reduce_fusion
  256.2 0.1 copy.38
  256.2 0.1 mul.270
  256.3 0.7 reshape.84
  257.0 3.2 all-to-all-start.2
  260.3 96.2 %while.14 = (s32[]{:T(128)}, f32[32,2,256,256]{3,2,0,1:T(8,128)}, bf16[4,32,256,2,16]{2,4,3,1,0:T(8,128)(2,1)S(1)}, s32[]{:T(128)}, s32[]{:T(128)}) while((s32[]{:T(128)}, f32[32,2,256,256]{3,2,0,1:T(8,128)}, bf16[4,32,256,2,16]{2,4,3,1,0:T(8,128)(2,1)S(1)}, s32[]{:T(128)}, s32[]{:T(128)}) %tuple.65), condition=%wide.region_1.2_spmd.clone, body=%wide.region_0.1_spmd.clone.sunk | while | flops 293994496 | bytes 72876112 | solution.py:93
  260.5 1.3 fusion.78
  261.8 3.2 fusion.79
  265.0 6.3 %pad_maximum_fusion.7 = bf16[32,2,256,256]{3,2,0,1:T(8,128)(2,1)} fusion(bf16[32,1,256,256]{3,2,0,1:T(8,128)(2,1)S(1)} %fusion.78, bf16[32,1,256,256]{3,2,0,1:T(8,128)(2,1)} %fusion.79), kind=kLoop, calls=%fused_computation.1.clone.1 | loop fusion | flops 4194304 | bytes 16777216 | tf_op jit(solution)/shard_map/while/body/eval_jaxpr/stack | solution.py:88
  271.4 9.9 %select_add_fusion.2 = f32[32,2,256,256]{3,2,0,1:T(8,128)} fusion(f32[32,2,256,256]{3,2,0,1:T(8,128)} %get-tuple-element.149, bf16[32,2,256,256]{3,2,0,1:T(8,128)(2,1)} %pad_maximum_fusion.7, pred[]{:T(512)S(6)} %compare.4), kind=kLoop, calls=%fused_computation.clone.1 | loop fusion | flops 12582912 | bytes 41943040 | tf_op jit(solution)/shard_map/while/body/eval_jaxpr/add | solution.py:90
  281.5 1.3 fusion.78
  282.8 3.2 fusion.79
  286.1 6.3 %pad_maximum_fusion.7 = bf16[32,2,256,256]{3,2,0,1:T(8,128)(2,1)} fusion(bf16[32,1,256,256]{3,2,0,1:T(8,128)(2,1)S(1)} %fusion.78, bf16[32,1,256,256]{3,2,0,1:T(8,128)(2,1)} %fusion.79), kind=kLoop, calls=%fused_computation.1.clone.1 | loop fusion | flops 4194304 | bytes 16777216 | tf_op jit(solution)/shard_map/while/body/eval_jaxpr/stack | solution.py:88
  292.4 14.0 %select_add_fusion.2 = f32[32,2,256,256]{3,2,0,1:T(8,128)} fusion(f32[32,2,256,256]{3,2,0,1:T(8,128)} %get-tuple-element.149, bf16[32,2,256,256]{3,2,0,1:T(8,128)(2,1)} %pad_maximum_fusion.7, pred[]{:T(512)S(6)} %compare.4), kind=kLoop, calls=%fused_computation.clone.1 | loop fusion | flops 12582912 | bytes 41943040 | tf_op jit(solution)/shard_map/while/body/eval_jaxpr/add | solution.py:90
  306.6 1.3 fusion.78
  307.9 3.2 fusion.79
  311.1 6.3 %pad_maximum_fusion.7 = bf16[32,2,256,256]{3,2,0,1:T(8,128)(2,1)} fusion(bf16[32,1,256,256]{3,2,0,1:T(8,128)(2,1)S(1)} %fusion.78, bf16[32,1,256,256]{3,2,0,1:T(8,128)(2,1)} %fusion.79), kind=kLoop, calls=%fused_computation.1.clone.1 | loop fusion | flops 4194304 | bytes 16777216 | tf_op jit(solution)/shard_map/while/body/eval_jaxpr/stack | solution.py:88
  317.5 14.0 %select_add_fusion.2 = f32[32,2,256,256]{3,2,0,1:T(8,128)} fusion(f32[32,2,256,256]{3,2,0,1:T(8,128)} %get-tuple-element.149, bf16[32,2,256,256]{3,2,0,1:T(8,128)(2,1)} %pad_maximum_fusion.7, pred[]{:T(512)S(6)} %compare.4), kind=kLoop, calls=%fused_computation.clone.1 | loop fusion | flops 12582912 | bytes 41943040 | tf_op jit(solution)/shard_map/while/body/eval_jaxpr/add | solution.py:90
  331.6 1.3 fusion.78
  332.9 3.2 fusion.79
  336.2 6.3 %pad_maximum_fusion.7 = bf16[32,2,256,256]{3,2,0,1:T(8,128)(2,1)} fusion(bf16[32,1,256,256]{3,2,0,1:T(8,128)(2,1)S(1)} %fusion.78, bf16[32,1,256,256]{3,2,0,1:T(8,128)(2,1)} %fusion.79), kind=kLoop, calls=%fused_computation.1.clone.1 | loop fusion | flops 4194304 | bytes 16777216 | tf_op jit(solution)/shard_map/while/body/eval_jaxpr/stack | solution.py:88
  342.5 14.0 %select_add_fusion.2 = f32[32,2,256,256]{3,2,0,1:T(8,128)} fusion(f32[32,2,256,256]{3,2,0,1:T(8,128)} %get-tuple-element.149, bf16[32,2,256,256]{3,2,0,1:T(8,128)(2,1)} %pad_maximum_fusion.7, pred[]{:T(512)S(6)} %compare.4), kind=kLoop, calls=%fused_computation.clone.1 | loop fusion | flops 12582912 | bytes 41943040 | tf_op jit(solution)/shard_map/while/body/eval_jaxpr/add | solution.py:90
  356.5 11.7 %copy.41 = f32[32,2,256,256]{3,2,1,0:T(8,128)} copy(f32[32,2,256,256]{3,2,0,1:T(8,128)} %get-tuple-element.94) | data formatting | bytes 33554432
  368.2 0.0 all-to-all-done.2
  368.2 0.5 broadcast.40
  368.7 0.7 reduce.1
  369.4 0.1 reshape.85
  369.5 0.7 squeeze.11
  (20 shorter events, 0.7 us)
Async XLA Ops:
  0.6 50.8 %copy-start = (bf16[16,32,2048]{2,1,0:T(8,128)(2,1)S(1)}, bf16[16,32,2048]{2,1,0:T(8,128)(2,1)}, u32[]{:S(2)}) copy-start(bf16[16,32,2048]{2,1,0:T(8,128)(2,1)} %param.5) | copy-start | bytes 6291460
  3.8 45.8 %collective-permute-start = (bf16[15,32,2048]{2,1,0:T(8,128)(2,1)}, bf16[15,32,2048]{2,1,0:T(8,128)(2,1)}, u32[]{:S(2)}, u32[]{:S(2)}) collective-permute-start(bf16[15,32,2048]{2,1,0:T(8,128)(2,1)} %slice.112), channel_id=1, source_target_pairs={{0,1},{1,2},{2,3},{4,5},{5,6},{6,7},{8,9},{9,10},{10,11},{12,13},{... | collective-permute-start | bytes 5898248 | tf_op jit(solution)/shard_map/ppermute | solution.py:12
  202.5 53.2 %all-to-all-start.1 = ((bf16[1,128,256,2,16]{2,4,3,0,1:T(8,128)(2,1)}), bf16[1,128,256,2,16]{2,4,3,0,1:T(8,128)(2,1)S(1)}, u32[]{:S(2)}, u32[]{:S(2)}) async-start(bf16[1,128,256,2,16]{2,4,3,0,1:T(8,128)(2,1)} %copy.36), calls=%async_computation.1 | async-start | bytes 4194304 | tf_op jit(solution)/shard_map/all_to_all | solution.py:72
  257.0 111.1 %all-to-all-start.2 = ((f32[4,1,512]{2,1,0:T(1,128)}), f32[4,1,512]{2,1,0:T(1,128)S(1)}, u32[]{:S(2)}, u32[]{:S(2)}) async-start(f32[4,1,512]{2,1,0:T(1,128)} %reshape.84), calls=%async_computation.2 | async-start | bytes 16384 | tf_op jit(solution)/shard_map/all_to_all | solution.py:82
where the time goes:
time: 373 us; the launch traced here: 370 us
  other arithmetic  90.2 us (24%)
  waiting for transfers between devices  86.6 us (23%)
  matrix products  82.4 us (22%)
  local copies, waits for them, and re-layouts  65.6 us (18%)
  blocking collectives  30.4 us (8%)
  starting transfers between devices  14.1 us (4%)
    add x4, other arithmetic, accumulate(): return running + partial_value.astype(jnp.float32)  51.9 us
    all_to_all x1, waiting for transfers between devices, body(): lax.all_to_all(lax.all_to_all(spectra[None], 'station', split_axis=1, con...  47.7 us
    ppermute x1, waiting for transfers between devices, passed_along(): return lax.ppermute(block, axis, route)  38.9 us
    dot_general x1, matrix products, body(): jnp.einsum('nc,atn->cat', sin_part, weighted, preferred_element_type=jnp....  32.5 us
    dot_general x1, matrix products, body(): jnp.einsum('nc,atn->cat', cos_part, weighted, preferred_element_type=jnp....  31.8 us
    unnamed x7, local copies, waits for them, and re-layouts  31.2 us
    all_to_all x1, blocking collectives, body(): lax.all_to_all(spectra[None], 'station', split_axis=1, concat_axis=2, til...  30.4 us
    another operation x4, other arithmetic, accumulate(): jnp.stack([real_part, imag_part], axis=1).astype(jnp.bfloat16)  25.4 us
  transfers between devices with their start and end apart: 3, of which 2 were waited for; matrix products, arithmetic and copies ran while one was open for 30% of the time, Pallas kernels for 0%

commit v1 on v0

v1 whole, which is shorter than its diff:
```python
import functools
import math

import jax
import jax.numpy as jnp
from jax import lax
from jax.experimental import pallas as pl
from jax.experimental.pallas import tpu as pltpu
from jax.sharding import PartitionSpec as P

BOTH = ("station", "tm")
VMEM_LIMIT = 56 * 1024 * 1024


def passed_along(block, axis, distance):
    devices = range(lax.axis_size(axis))
    route = [(i - distance, i) for i in devices if i - distance in devices]
    return lax.ppermute(block, axis, route)


def angle_tables(rows, step, frame_len):
    row = jnp.arange(rows, dtype=jnp.int32) * step
    sample = jnp.arange(frame_len, dtype=jnp.int32)
    phases = row[:, None] * sample[None, :] % frame_len
    angles = phases.astype(jnp.float32) * (2.0 * math.pi / frame_len)
    return jnp.cos(angles), jnp.sin(angles)


def filter_frames(extended, taps, frames_out):
    span_taps = taps.shape[0]
    running = jnp.zeros((frames_out,) + extended.shape[1:], jnp.float32)
    for tap_index in range(span_taps):
        offset = span_taps - 1 - tap_index
        running = running + taps[tap_index][None, None, :] * extended[
            offset : offset + frames_out
        ].astype(jnp.float32)
    return running.astype(jnp.bfloat16)


def dft_kernel(own, cos_hi, sin_hi, cos_lo, sin_lo, weighted, pick, spec, power, table):
    group = cos_hi.shape[0]
    c_lo, s_lo = cos_lo[...], sin_lo[...]
    for g in range(group):
        c_hi, s_hi = cos_hi[g : g + 1], sin_hi[g : g + 1]
        real = c_hi * c_lo - s_hi * s_lo
        imag = -(s_hi * c_lo + c_hi * s_lo)
        table[g * 2 * own : (g + 1) * 2 * own] = jnp.concatenate([real, imag], axis=0).astype(
            jnp.bfloat16
        )
    out = lax.dot_general(
        table[...], weighted[...], (((1,), (1,)), ((), ())), preferred_element_type=jnp.float32
    )
    out = out.astype(jnp.bfloat16).reshape(group, 2 * own, out.shape[1])
    spec[...] = out
    values = out.astype(jnp.float32)
    values = values * values
    total = (values[:, :own] + values[:, own:]).reshape(group * own, out.shape[2])
    power[...] = lax.dot_general(
        pick[...],
        total,
        (((1,), (1,)), ((), ())),
        precision=lax.Precision.HIGHEST,
        preferred_element_type=jnp.float32,
    )


def channelise(weighted, own, frames, dests):
    rows, frame_len = weighted.shape
    group = max(1, min(dests, 512 // (2 * own)))
    cos_hi, sin_hi = angle_tables(dests, own, frame_len)
    cos_lo, sin_lo = angle_tables(own, 1, frame_len)
    column = jnp.arange(rows, dtype=jnp.int32) // (rows // frames)
    pick = (column[None, :] == jnp.arange(frames, dtype=jnp.int32)[:, None]).astype(jnp.float32)
    whole = lambda a: pl.BlockSpec(a.shape, lambda i: (0, 0))
    high = pl.BlockSpec((group, frame_len), lambda i: (i, 0))
    return pl.pallas_call(
        functools.partial(dft_kernel, own),
        grid=(dests // group,),
        in_specs=[high, high, whole(cos_lo), whole(sin_lo), whole(weighted), whole(pick)],
        out_specs=[
            pl.BlockSpec((group, 2 * own, rows), lambda i: (i, 0, 0)),
            pl.BlockSpec((frames, group * own), lambda i: (0, i)),
        ],
        out_shape=[
            jax.ShapeDtypeStruct((dests, 2 * own, rows), jnp.bfloat16),
            jax.ShapeDtypeStruct((frames, dests * own), jnp.float32),
        ],
        scratch_shapes=[pltpu.VMEM((group * 2 * own, frame_len), jnp.bfloat16)],
        compiler_params=pltpu.CompilerParams(vmem_limit_bytes=VMEM_LIMIT),
    )(cos_hi, sin_hi, cos_lo, sin_lo, weighted, pick)


def correlate_kernel(stations, blocks, own, local, scale, got, vis, wide):
    chunks = got.shape[2] // 128
    slots = 128 // local
    channel = pl.program_id(0)

    @pl.when(channel == 0)
    def _():
        def fill(s, carry):
            for tm in range(blocks):
                for p in range(2):
                    piece = got[s * blocks + tm, p * own : (p + 1) * own, :].astype(jnp.float32)
                    base = (p * blocks + tm) * own
                    for j in range(chunks):
                        wide[s * chunks + j, base : base + own, :] = piece[
                            :, j * 128 : (j + 1) * 128
                        ]
            return carry

        lax.fori_loop(0, stations, fill, 0)

    rows = 2 * blocks
    lane = lax.broadcasted_iota(jnp.int32, (rows, 128), 1) // local
    sign = jnp.where(lax.broadcasted_iota(jnp.int32, (rows, 256), 0) < blocks, 1.0, -1.0)
    flat, turned = [], []
    for j in range(chunks):
        halves = []
        for h in range(stations // slots):
            parts = [
                wide[(h * slots + s) * chunks + j, pl.ds(channel, rows, stride=own), :]
                for s in range(slots)
            ]
            tiles = []
            for t in range(slots):
                tile = None
                for s in range(slots):
                    shift = (s - t) % slots * local
                    moved = parts[s] if shift == 0 else pltpu.roll(parts[s], shift, 1)
                    tile = moved if tile is None else jnp.where(lane == s, moved, tile)
                tiles.append(tile)
            halves.append(tiles)
        for t in range(slots):
            full = jnp.concatenate([half[t] for half in halves], axis=1)
            flat.append(full)
            turned.append(pltpu.roll(full, blocks, 0) * sign)
    flat = jnp.concatenate(flat, axis=0).astype(jnp.bfloat16)
    turned = jnp.concatenate(turned, axis=0).astype(jnp.bfloat16)
    over_rows = (((0,), (0,)), ((), ()))
    vis[0, 0] = lax.dot_general(flat, flat, over_rows, preferred_element_type=jnp.float32) * scale
    vis[0, 1] = lax.dot_general(flat, turned, over_rows, preferred_element_type=jnp.float32) * scale


def correlate(got, stations, blocks, own, local, scale):
    inputs = stations * local
    chunks = got.shape[2] // 128
    return pl.pallas_call(
        functools.partial(correlate_kernel, stations, blocks, own, local, scale),
        grid=(own,),
        in_specs=[pl.BlockSpec(got.shape, lambda c: (0, 0, 0))],
        out_specs=pl.BlockSpec((1, 2, inputs, inputs), lambda c: (c, 0, 0, 0)),
        out_shape=jax.ShapeDtypeStruct((own, 2, inputs, inputs), jnp.float32),
        scratch_shapes=[pltpu.VMEM((stations * chunks, 2 * blocks * own, 128), jnp.float32)],
        compiler_params=pltpu.CompilerParams(vmem_limit_bytes=VMEM_LIMIT),
    )(got)


def body(samples, history, taps):
    frames_dev, local, frame_len = samples.shape
    span_taps = taps.shape[0]
    stations, blocks = lax.axis_size("station"), lax.axis_size("tm")
    dests = stations * blocks
    own = frame_len // 2 // dests
    tail_block = samples[frames_dev - (span_taps - 1) :]
    prior_frames = passed_along(tail_block, "tm", 1)
    prior_frames = jnp.where(lax.axis_index("tm") == 0, history, prior_frames)
    extended = jnp.concatenate([prior_frames, samples], axis=0)
    weighted = filter_frames(extended, taps, frames_dev).reshape(frames_dev * local, frame_len)
    spectra, power = channelise(weighted, own, frames_dev, dests)
    got = lax.all_to_all(spectra, BOTH, split_axis=0, concat_axis=0, tiled=True)
    power = lax.psum_scatter(power, "station", scatter_dimension=1, tiled=True)
    power = power * (1.0 / (stations * local))
    visibility = correlate(got, stations, blocks, own, local, 1.0 / (frames_dev * blocks))
    return visibility, power


def solution(mesh):
    return jax.shard_map(
        body,
        mesh=mesh,
        in_specs=(P("tm", "station", None), P(None, "station", None), P()),
        out_specs=(P(("station", "tm"), None, None, None), P("tm", "station")),
        check_vma=False,
    )
```

time: 373 us -> 166 us (0.45)
  matrix products: 82.4 us -> 0 us
  other arithmetic: 90.2 us -> 17.6 us
  local copies, waits for them, and re-layouts: 65.6 us -> 4.51 us
  Pallas kernels: 0 us -> 32.8 us
  blocking collectives: 30.4 us -> 0 us
  between operations: 0.74 us -> 14.1 us
    dot_general x10 -> x0, matrix products: 82.4 us -> none  [the longest x1 32.5 us: body(): jnp.einsum('nc,atn->cat', sin_part, weighted, preferred_element_type=jnp....]
    add x4 -> x0, other arithmetic: 51.9 us -> none  [accumulate(): return running + partial_value.astype(jnp.float32)]
    all_to_all x2 -> x1, waiting for transfers between devices: 47.7 us -> 10 us  [body(): got = lax.all_to_all(spectra, BOTH, split_axis=0, concat_axis=0, tiled=True)]
    reduce_scatter x0 -> x1, waiting for transfers between devices: none -> 36.2 us  [body(): power = lax.psum_scatter(power, 'station', scatter_dimension=1, tiled=True)]
    pallas_call x0 -> x2, Pallas kernels: none -> 32.8 us  [the longest x1 21.6 us: correlate(): pl.pallas_call(functools.partial(correlate_kernel, stations, blocks, own,...]
    all_to_all x1 -> x0, blocking collectives: 30.4 us -> none  [body(): lax.all_to_all(spectra[None], 'station', split_axis=1, concat_axis=2, til...]
    unnamed x7 -> x6, local copies, waits for them, and re-layouts: 31.2 us -> 1.34 us
    another operation x5 -> x0, other arithmetic: 25.6 us -> none  [the longest x4 25.4 us: accumulate(): jnp.stack([real_part, imag_part], axis=1).astype(jnp.bfloat16)]
  transfers between devices with their start and end apart: 3 -> 3, of which waited for: 2 -> 3; matrix products, arithmetic and copies ran while one was open for 30% -> 3% of each run, Pallas kernels for 0% -> 0%
where the time goes in v1:
time: 166 us; the launch traced here: 165 us
  waiting for transfers between devices  82.9 us (50%)
  Pallas kernels  32.8 us (20%)
  other arithmetic  17.6 us (11%)
  between operations  14.1 us (8%)
  starting transfers between devices  13.5 us (8%)
  local copies, waits for them, and re-layouts  4.51 us (3%)
    reduce_scatter x1, waiting for transfers between devices, body(): power = lax.psum_scatter(power, 'station', scatter_dimension=1, tiled=True)  36.2 us
    ppermute x1, waiting for transfers between devices, passed_along(): return lax.ppermute(block, axis, route)  36.1 us
    pallas_call x1, Pallas kernels, correlate(): pl.pallas_call(functools.partial(correlate_kernel, stations, blocks, own,...  21.6 us
    pallas_call x1, Pallas kernels, channelise(): pl.pallas_call(functools.partial(dft_kernel, own), grid=(dests // group,)...  11.3 us
    convert_element_type x1, other arithmetic, filter_frames(): return running.astype(jnp.bfloat16)  10.2 us
    all_to_all x1, waiting for transfers between devices, body(): got = lax.all_to_all(spectra, BOTH, split_axis=0, concat_axis=0, tiled=True)  10 us
    all_to_all x1, starting transfers between devices, body(): got = lax.all_to_all(spectra, BOTH, split_axis=0, concat_axis=0, tiled=True)  8.04 us
    ppermute x1, starting transfers between devices, passed_along(): return lax.ppermute(block, axis, route)  5.46 us
  transfers between devices with their start and end apart: 3, of which 3 were waited for; matrix products, arithmetic and copies ran while one was open for 3% of the time, Pallas kernels for 0%

profile of v1, /device:TPU:1, one launch (start us, length us, event | category | flops | bytes accessed | tf_op | source)
XLA Modules:
  0.0 165.5 jit_solution(7871169471003620112)
XLA Ops:
  7.2 0.0 copy-start.2
  7.2 3.1 %slice.98 = bf16[15,32,2048]{2,1,0:T(8,128)(2,1)} slice(bf16[16,32,2048]{2,1,0:T(8,128)(2,1)} %param.3), slice={[1:16], [0:32], [0:2048]} | slice | bytes 3932160 | tf_op jit(solution)/shard_map/slice | solution.py:164
  10.3 0.0 copy-start.1
  10.3 5.5 %collective-permute-start = (bf16[15,32,2048]{2,1,0:T(8,128)(2,1)}, bf16[15,32,2048]{2,1,0:T(8,128)(2,1)}, u32[]{:S(2)}, u32[]{:S(2)}) collective-permute-start(bf16[15,32,2048]{2,1,0:T(8,128)(2,1)} %slice.98), channel_id=1, source_target_pairs={{0,1},{1,2},{2,3},{4,5},{5,6},{6,7},{8,9},{9,10},{10,11},{12,13},{... | collective-permute-start | bytes 5898248 | tf_op jit(solution)/shard_map/ppermute | solution.py:18
  15.7 0.6 fusion.30.pick
  16.3 1.8 %fusion.26 = (f32[32,2048]{1,0:T(8,128)}, f32[32,2048]{1,0:T(8,128)}) fusion(), kind=kLoop, calls=%fused_computation.63 | loop fusion | flops 917504 | bytes 524288 | tf_op jit(solution)/shard_map/sin | solution.py:26
  18.1 0.0 copy-done.2
  18.1 0.1 fusion.34
  18.2 1.9 %fusion.28 = (f32[32,2048]{1,0:T(8,128)}, f32[32,2048]{1,0:T(8,128)}) fusion(s32[32]{0:T(128)S(1)} %iota_multiply_fusion), kind=kLoop, calls=%fused_computation.65 | loop fusion | flops 917504 | bytes 524416 | tf_op jit(solution)/shard_map/sin | solution.py:26
  20.1 36.1 %collective-permute-done = bf16[15,32,2048]{2,1,0:T(8,128)(2,1)} collective-permute-done((bf16[15,32,2048]{2,1,0:T(8,128)(2,1)}, bf16[15,32,2048]{2,1,0:T(8,128)(2,1)}, u32[]{:S(2)}, u32[]{:S(2)}) %collective-permute-start) | collective-permute-done | bytes 1966112 | tf_op jit(solution)/shard_map/ppermute | solution.py:18
  56.2 1.8 %broadcast_select_fusion = bf16[15,32,2048]{2,1,0:T(8,128)(2,1)S(1)} fusion(bf16[15,32,2048]{2,1,0:T(8,128)(2,1)} %param.4, bf16[15,32,2048]{2,1,0:T(8,128)(2,1)} %collective-permute-done, pred[]{:T(512)S(6)} %eq.19), kind=kLoop, calls=%fused_computation.44 | loop fusion | flops 983040 | bytes 5898241 | tf_op jit(solution)/shard_map/jit(_where)/select_n | solution.py:166
  58.0 0.0 copy-done.1
  58.0 10.2 %add_convert_fusion = bf16[16,32,2048]{2,1,0:T(8,128)(2,1)} fusion(bf16[16,32,2048]{2,1,0:T(8,128)(2,1)S(1)} %copy-done.1, bf16[15,32,2048]{2,1,0:T(8,128)(2,1)S(1)} %broadcast_select_fusion, f32[2048]{0:T(1024)S(1)} %bitcast.32, f32[2048]{0:T(1024)S(1)} %bitcast.33, f32[2048]{0:T(1024)S(1)} %bitcast.19, f32[2048]{0:T(1024)S(1)} %bitcast.20, ...), kind=kLoop, calls=%fused_computation.28 | loop fusion | flops 66060288 | bytes 6291456 | tf_op jit(solution)/shard_map/convert_element_type | solution.py:37
  68.1 11.3 %shard_map.50 = (bf16[32,64,512]{2,1,0:T(8,128)(2,1)}, f32[16,1024]{1,0:T(8,128)}) custom-call(f32[32,2048]{1,0:T(8,128)} %get-tuple-element.23.cos_hi, f32[32,2048]{1,0:T(8,128)} %get-tuple-element.22.sin_hi, f32[32,2048]{1,0:T(8,128)} %get-tuple-element.25.cos_lo, f32[32,2048]{1,0:T(8,128)} %get-tuple-element.24.sin_lo, bf16[512,2048]{1,0:T(8,128)(2,1)} %bitcast.17, ...), custom_call_target="tpu_custom_call" | custom-call | tf_op jit(solution)/shard_map/pallas_call | solution.py:76
  79.4 8.0 %all-to-all-start = ((bf16[32,64,512]{2,1,0:T(8,128)(2,1)}), bf16[32,64,512]{2,1,0:T(8,128)(2,1)S(1)}, u32[]{:S(2)}, u32[]{:S(2)}) async-start(bf16[32,64,512]{2,1,0:T(8,128)(2,1)} %get-tuple-element.4), calls=%async_computation | async-start | bytes 4194304 | tf_op jit(solution)/shard_map/all_to_all | solution.py:170
  87.5 0.0 reduce-scatter.2.cloned.1.call-start
  87.5 0.7 reduce-scatter.2.cloned.1.call-update
  88.2 36.2 %reduce-scatter.2.cloned.1.call-done = f32[16,128]{1,0:T(8,128)} async-done(((f32[16,1024]{1,0:T(8,128)}), f32[16,128]{1,0:T(8,128)}) %reduce-scatter.2.cloned.1.call-update) | async-done | bytes 8208 | tf_op jit(solution)/shard_map/reduce_scatter | solution.py:171
  124.4 1.3 broadcast_multiply_fusion
  125.7 10.0 %all-to-all-done.got = bf16[32,64,512]{2,1,0:T(8,128)(2,1)S(1)} async-done(((bf16[32,64,512]{2,1,0:T(8,128)(2,1)}), bf16[32,64,512]{2,1,0:T(8,128)(2,1)S(1)}, u32[]{:S(2)}, u32[]{:S(2)}) %all-to-all-start) | async-done | bytes 2097184 | tf_op jit(solution)/shard_map/all_to_all | solution.py:170
  135.7 0.0 copy-start
  135.7 1.3 copy-done
  137.0 21.6 %shard_map.51 = f32[32,2,256,256]{3,2,1,0:T(8,128)} custom-call(bf16[32,64,512]{2,1,0:T(8,128)(2,1)} %copy-done), custom_call_target="tpu_custom_call" | custom-call | tf_op jit(solution)/shard_map/pallas_call | solution.py:147
  (2 shorter events, 0.0 us)
Async XLA Ops:
  7.2 10.9 %copy-start.2 = (f32[16,2048]{1,0:T(8,128)S(1)}, f32[16,2048]{1,0:T(8,128)}, u32[]{:S(2)}) copy-start(f32[16,2048]{1,0:T(8,128)} %param.5) | copy-start | bytes 393220
  10.3 47.7 %copy-start.1 = (bf16[16,32,2048]{2,1,0:T(8,128)(2,1)S(1)}, bf16[16,32,2048]{2,1,0:T(8,128)(2,1)}, u32[]{:S(2)}) copy-start(bf16[16,32,2048]{2,1,0:T(8,128)(2,1)} %param.3) | copy-start | bytes 6291460
  10.3 45.9 %collective-permute-start = (bf16[15,32,2048]{2,1,0:T(8,128)(2,1)}, bf16[15,32,2048]{2,1,0:T(8,128)(2,1)}, u32[]{:S(2)}, u32[]{:S(2)}) collective-permute-start(bf16[15,32,2048]{2,1,0:T(8,128)(2,1)} %slice.98), channel_id=1, source_target_pairs={{0,1},{1,2},{2,3},{4,5},{5,6},{6,7},{8,9},{9,10},{10,11},{12,13},{... | collective-permute-start | bytes 5898248 | tf_op jit(solution)/shard_map/ppermute | solution.py:18
  79.4 56.3 %all-to-all-start = ((bf16[32,64,512]{2,1,0:T(8,128)(2,1)}), bf16[32,64,512]{2,1,0:T(8,128)(2,1)S(1)}, u32[]{:S(2)}, u32[]{:S(2)}) async-start(bf16[32,64,512]{2,1,0:T(8,128)(2,1)} %get-tuple-element.4), calls=%async_computation | async-start | bytes 4194304 | tf_op jit(solution)/shard_map/all_to_all | solution.py:170
  87.5 36.9 %reduce-scatter.2.cloned.1.call-start = ((), (), s32[]{:S(2)}) async-start(), calls=%async_computation.2 | async-start | bytes 73728 | tf_op jit(solution)/shard_map/reduce_scatter | solution.py:171
  135.7 1.3 copy-start
Sparse Core Ops, SparseCore 0:
  91.3 33.0 reduce-scatter.1

commit v2 on v1

v2 whole, which is shorter than its diff:
```python
import functools
import math

import jax
import jax.numpy as jnp
from jax import lax
from jax.experimental import pallas as pl
from jax.experimental.pallas import tpu as pltpu
from jax.sharding import PartitionSpec as P

BOTH = ("station", "tm")
VMEM_LIMIT = 56 * 1024 * 1024


def passed_along(block, axis, distance):
    devices = range(lax.axis_size(axis))
    route = [(i - distance, i) for i in devices if i - distance in devices]
    return lax.ppermute(block, axis, route)


def angle_tables(rows, step, frame_len):
    row = jnp.arange(rows, dtype=jnp.int32) * step
    sample = jnp.arange(frame_len, dtype=jnp.int32)
    phases = row[:, None] * sample[None, :] % frame_len
    angles = phases.astype(jnp.float32) * (2.0 * math.pi / frame_len)
    return jnp.cos(angles), jnp.sin(angles)


def filter_frames(extended, taps, frames_out):
    span_taps = taps.shape[0]
    running = jnp.zeros((frames_out,) + extended.shape[1:], jnp.float32)
    for tap_index in range(span_taps):
        offset = span_taps - 1 - tap_index
        running = running + taps[tap_index][None, None, :] * extended[
            offset : offset + frames_out
        ].astype(jnp.float32)
    return running.astype(jnp.bfloat16)


def table_kernel(own, cos_hi, sin_hi, cos_lo, sin_lo, table):
    c_lo, s_lo = cos_lo[...], sin_lo[...]
    for g in range(cos_hi.shape[0]):
        c_hi, s_hi = cos_hi[g : g + 1], sin_hi[g : g + 1]
        real = c_hi * c_lo - s_hi * s_lo
        imag = -(s_hi * c_lo + c_hi * s_lo)
        table[g * 2 * own : (g + 1) * 2 * own] = jnp.concatenate([real, imag], axis=0).astype(
            jnp.bfloat16
        )


def dft_table(own, dests, group, frame_len):
    cos_hi, sin_hi = angle_tables(dests, own, frame_len)
    cos_lo, sin_lo = angle_tables(own, 1, frame_len)
    high = pl.BlockSpec((group, frame_len), lambda i: (i, 0))
    low = pl.BlockSpec((own, frame_len), lambda i: (0, 0))
    return pl.pallas_call(
        functools.partial(table_kernel, own),
        grid=(dests // group,),
        in_specs=[high, high, low, low],
        out_specs=pl.BlockSpec((group * 2 * own, frame_len), lambda i: (i, 0)),
        out_shape=jax.ShapeDtypeStruct((dests * 2 * own, frame_len), jnp.bfloat16),
        compiler_params=pltpu.CompilerParams(vmem_limit_bytes=VMEM_LIMIT),
        cost_estimate=pl.CostEstimate(
            flops=dests * own * frame_len * 8,
            bytes_accessed=dests * own * frame_len * 4,
            transcendentals=0,
        ),
    )(cos_hi, sin_hi, cos_lo, sin_lo)


def dft_kernel(own, table, weighted, pick, spec, power):
    group = spec.shape[0]
    out = lax.dot_general(
        table[...], weighted[...], (((1,), (1,)), ((), ())), preferred_element_type=jnp.float32
    )
    out = out.astype(jnp.bfloat16).reshape(group, 2 * own, out.shape[1])
    spec[...] = out
    values = out.astype(jnp.float32)
    values = values * values
    total = (values[:, :own] + values[:, own:]).reshape(group * own, out.shape[2])
    power[...] = lax.dot_general(
        pick[...],
        total,
        (((1,), (1,)), ((), ())),
        precision=lax.Precision.HIGHEST,
        preferred_element_type=jnp.float32,
    )


def channelise(table, weighted, own, frames, dests, group):
    rows, frame_len = weighted.shape
    column = jnp.arange(rows, dtype=jnp.int32) // (rows // frames)
    pick = (column[None, :] == jnp.arange(frames, dtype=jnp.int32)[:, None]).astype(jnp.float32)
    return pl.pallas_call(
        functools.partial(dft_kernel, own),
        grid=(dests // group,),
        in_specs=[
            pl.BlockSpec((group * 2 * own, frame_len), lambda i: (i, 0)),
            pl.BlockSpec((rows, frame_len), lambda i: (0, 0)),
            pl.BlockSpec((frames, rows), lambda i: (0, 0)),
        ],
        out_specs=[
            pl.BlockSpec((group, 2 * own, rows), lambda i: (i, 0, 0)),
            pl.BlockSpec((frames, group * own), lambda i: (0, i)),
        ],
        out_shape=[
            jax.ShapeDtypeStruct((dests, 2 * own, rows), jnp.bfloat16),
            jax.ShapeDtypeStruct((frames, dests * own), jnp.float32),
        ],
        compiler_params=pltpu.CompilerParams(vmem_limit_bytes=VMEM_LIMIT),
        cost_estimate=pl.CostEstimate(
            flops=4 * dests * own * frame_len * rows,
            bytes_accessed=dests * own * frame_len * 4,
            transcendentals=0,
        ),
    )(table, weighted, pick)


def channel_rows(wide, channel, stations, blocks, own, local):
    chunks = wide.shape[0] // stations
    slots = 128 // local
    rows = 2 * blocks
    lane = lax.broadcasted_iota(jnp.int32, (rows, 128), 1) // local
    sign = jnp.where(
        lax.broadcasted_iota(jnp.int32, (rows, stations * local), 0) < blocks, 1.0, -1.0
    )
    flat, turned = [], []
    for j in range(chunks):
        halves = []
        for h in range(stations // slots):
            parts = [
                wide[(h * slots + s) * chunks + j, pl.ds(channel, rows, stride=own), :]
                for s in range(slots)
            ]
            tiles = []
            for t in range(slots):
                tile = None
                for s in range(slots):
                    shift = (s - t) % slots * local
                    moved = parts[s] if shift == 0 else pltpu.roll(parts[s], shift, 1)
                    tile = moved if tile is None else jnp.where(lane == s, moved, tile)
                tiles.append(tile)
            halves.append(tiles)
        for t in range(slots):
            full = jnp.concatenate([half[t] for half in halves], axis=1)
            flat.append(full)
            turned.append(pltpu.roll(full, blocks, 0) * sign)
    flat = jnp.concatenate(flat, axis=0).astype(jnp.bfloat16)
    turned = jnp.concatenate(turned, axis=0).astype(jnp.bfloat16)
    return flat, turned


def correlate_kernel(stations, blocks, own, local, scale, *refs):
    *parts, vis, wide = refs
    chunks = parts[0].shape[2] // 128
    group = vis.shape[0]
    inputs = stations * local
    step = pl.program_id(0)

    @pl.when(step == 0)
    def _():
        def fill(s, carry):
            for i, got in enumerate(parts):
                for tm in range(blocks):
                    for p in range(2):
                        piece = got[s * blocks + tm, p * own : (p + 1) * own, :]
                        piece = piece.astype(jnp.float32)
                        base = (p * blocks + tm) * own
                        for j in range(chunks):
                            at = (s * len(parts) + i) * chunks + j
                            wide[at, base : base + own, :] = piece[:, j * 128 : (j + 1) * 128]
            return carry

        lax.fori_loop(0, stations, fill, 0)

    for g in range(group):
        flat, turned = channel_rows(wide, step * group + g, stations, blocks, own, local)
        both = jnp.concatenate([flat, turned], axis=1)
        out = lax.dot_general(
            flat, both, (((0,), (0,)), ((), ())), preferred_element_type=jnp.float32
        )
        vis[g, 0] = out[:, :inputs] * scale
        vis[g, 1] = out[:, inputs:] * scale


def correlate(parts, stations, blocks, own, local, scale):
    inputs = stations * local
    chunks = sum(got.shape[2] for got in parts) // 128
    group = math.gcd(own, 4)
    return pl.pallas_call(
        functools.partial(correlate_kernel, stations, blocks, own, local, scale),
        grid=(own // group,),
        in_specs=[pl.BlockSpec(got.shape, lambda c: (0, 0, 0)) for got in parts],
        out_specs=pl.BlockSpec((group, 2, inputs, inputs), lambda c: (c, 0, 0, 0)),
        out_shape=jax.ShapeDtypeStruct((own, 2, inputs, inputs), jnp.float32),
        scratch_shapes=[pltpu.VMEM((stations * chunks, 2 * blocks * own, 128), jnp.float32)],
        compiler_params=pltpu.CompilerParams(vmem_limit_bytes=VMEM_LIMIT),
    )(*parts)


def body(samples, history, taps):
    frames_dev, local, frame_len = samples.shape
    span = taps.shape[0] - 1
    stations, blocks = lax.axis_size("station"), lax.axis_size("tm")
    dests = stations * blocks
    own = frame_len // 2 // dests
    group = max(1, min(dests, 512 // (2 * own)))
    half = frames_dev // 2
    first = lax.axis_index("tm") == 0
    tail = samples[frames_dev - span :]

    near = passed_along(tail[half:], "tm", 1)
    table = dft_table(own, dests, group, frame_len)
    near, far_tail, table = lax.optimization_barrier((near, tail[:half], table))
    far = passed_along(far_tail, "tm", 1)
    near = jnp.where(first, history[half:], near)
    late = filter_frames(jnp.concatenate([near, samples], axis=0), taps, half)
    late = late.reshape(half * local, frame_len)
    spec_late, power_late = channelise(table, late, own, half, dests, group)
    got_late = lax.all_to_all(spec_late, BOTH, split_axis=0, concat_axis=0, tiled=True)

    far = jnp.where(first, history[:half], far)
    early = filter_frames(jnp.concatenate([far, near, samples[:half]], axis=0), taps, half)
    early = early.reshape(half * local, frame_len)
    spec_early, power_early = channelise(table, early, own, half, dests, group)
    got_early = lax.all_to_all(spec_early, BOTH, split_axis=0, concat_axis=0, tiled=True)

    power = jnp.concatenate([power_early, power_late], axis=0)
    power = lax.psum_scatter(power, "station", scatter_dimension=1, tiled=True)
    power = power * (1.0 / (stations * local))
    scale = 1.0 / (frames_dev * blocks)
    visibility = correlate((got_early, got_late), stations, blocks, own, local, scale)
    return visibility, power


def solution(mesh):
    return jax.shard_map(
        body,
        mesh=mesh,
        in_specs=(P("tm", "station", None), P(None, "station", None), P()),
        out_specs=(P(("station", "tm"), None, None, None), P("tm", "station")),
        check_vma=False,
    )
```

time: 166 us -> 147 us (0.89)
  waiting for transfers between devices: 82.9 us -> 53.9 us
  starting transfers between devices: 13.5 us -> 19 us
  Pallas kernels: 32.8 us -> 35.3 us
  other arithmetic: 17.6 us -> 19.5 us
    ppermute x1 -> x2, waiting for transfers between devices: 36.1 us -> 7.04 us  [passed_along(): return lax.ppermute(block, axis, route)]
    pallas_call x1, Pallas kernels: 21.6 us -> 12.5 us  [correlate(): pl.pallas_call(functools.partial(correlate_kernel, stations, blocks, own,...]
    pallas_call x0 -> x1, Pallas kernels: none -> 6.2 us  [dft_table(): pl.pallas_call(functools.partial(table_kernel, own), grid=(dests // group...]
    pallas_call x1 -> x2, Pallas kernels: 11.3 us -> 16.7 us  [channelise(): pl.pallas_call(functools.partial(dft_kernel, own), grid=(dests // group,)...]
    ppermute x1 -> x2, starting transfers between devices: 5.46 us -> 9.16 us  [passed_along(): return lax.ppermute(block, axis, route)]
    all_to_all x1 -> x2, starting transfers between devices: 8.04 us -> 9.82 us  [the longest x1 5.44 us: body(): lax.all_to_all(spec_late, BOTH, split_axis=0, concat_axis=0, tiled=True)]
    all_to_all x1 -> x2, waiting for transfers between devices: 10 us -> 11.3 us  [the longest x1 11.3 us: body(): lax.all_to_all(spec_late, BOTH, split_axis=0, concat_axis=0, tiled=True)]
    convert_element_type x1 -> x2, other arithmetic: 10.2 us -> 10.6 us  [filter_frames(): return running.astype(jnp.bfloat16)]
  transfers between devices with their start and end apart: 3 -> 5, of which waited for: 3 -> 3; matrix products, arithmetic and copies ran while one was open for 3% -> 14% of each run, Pallas kernels for 0% -> 16%
where the time goes in v2:
time: 147 us; the launch traced here: 145 us
  waiting for transfers between devices  53.9 us (37%)
  Pallas kernels  35.3 us (24%)
  other arithmetic  19.5 us (13%)
  starting transfers between devices  19 us (13%)
  between operations  14.1 us (10%)
  local copies, waits for them, and re-layouts  3.6 us (2%)
    reduce_scatter x1, waiting for transfers between devices, body(): power = lax.psum_scatter(power, 'station', scatter_dimension=1, tiled=True)  35.5 us
    pallas_call x2, Pallas kernels, channelise(): pl.pallas_call(functools.partial(dft_kernel, own), grid=(dests // group,)...  16.7 us
    pallas_call x1, Pallas kernels, correlate(): pl.pallas_call(functools.partial(correlate_kernel, stations, blocks, own,...  12.5 us
    all_to_all x1, waiting for transfers between devices, body(): lax.all_to_all(spec_late, BOTH, split_axis=0, concat_axis=0, tiled=True)  11.3 us
    convert_element_type x2, other arithmetic, filter_frames(): return running.astype(jnp.bfloat16)  10.6 us
    ppermute x2, starting transfers between devices, passed_along(): return lax.ppermute(block, axis, route)  9.16 us
    ppermute x2, waiting for transfers between devices, passed_along(): return lax.ppermute(block, axis, route)  7.04 us
    pallas_call x1, Pallas kernels, dft_table(): pl.pallas_call(functools.partial(table_kernel, own), grid=(dests // group...  6.2 us
  transfers between devices with their start and end apart: 5, of which 3 were waited for; matrix products, arithmetic and copies ran while one was open for 14% of the time, Pallas kernels for 16%

profile of v2, /device:TPU:1, one launch (start us, length us, event | category | flops | bytes accessed | tf_op | source)
XLA Modules:
  0.0 145.5 jit_solution(7008973402445889191)
XLA Ops:
  7.2 1.2 slice.182
  8.4 4.1 %collective-permute-start = (bf16[7,32,2048]{2,1,0:T(8,128)(2,1)S(1)}, bf16[7,32,2048]{2,1,0:T(8,128)(2,1)S(1)}, u32[]{:S(2)}, u32[]{:S(2)}) collective-permute-start(bf16[7,32,2048]{2,1,0:T(8,128)(2,1)S(1)} %slice.182), channel_id=1, source_target_pairs={{0,1},{1,2},{2,3},{4,5},{5,6},{6,7},{8,9},{9,10},{10,11},{12,13},{... | collective-permute-start | bytes 2752520 | tf_op jit(solution)/shard_map/ppermute | solution.py:18
  12.5 1.8 %fusion.55 = (f32[32,2048]{1,0:T(8,128)}, f32[32,2048]{1,0:T(8,128)}) fusion(), kind=kLoop, calls=%fused_computation.104 | loop fusion | flops 917504 | bytes 524288 | tf_op jit(solution)/shard_map/sin | solution.py:26
  14.3 0.6 fusion.59.pick
  14.9 1.9 %fusion.57 = (f32[32,2048]{1,0:T(8,128)}, f32[32,2048]{1,0:T(8,128)}) fusion(s32[32]{0:T(128)S(1)} %iota_multiply_fusion), kind=kLoop, calls=%fused_computation.106 | loop fusion | flops 917504 | bytes 524416 | tf_op jit(solution)/shard_map/sin | solution.py:26
  16.8 0.0 copy-start.3
  16.8 0.0 copy-start
  16.9 6.2 %shard_map.50.table = bf16[2048,2048]{1,0:T(8,128)(2,1)} custom-call(f32[32,2048]{1,0:T(8,128)} %get-tuple-element.35.cos_hi, f32[32,2048]{1,0:T(8,128)} %get-tuple-element.34.sin_hi, f32[32,2048]{1,0:T(8,128)} %get-tuple-element.37.cos_lo, f32[32,2048]{1,0:T(8,128)} %get-tuple-element.36.sin_lo), custom_call_target="tpu_custom_call" | custom-call | flops 16777216 | bytes 8388608 | tf_op jit(solution)/shard_map/pallas_call | solution.py:56
  23.1 0.0 copy-done.3
  23.1 0.1 fusion.61
  23.1 0.0 copy-done
  23.2 1.3 fusion.60
  24.4 7.0 %collective-permute-done = bf16[7,32,2048]{2,1,0:T(8,128)(2,1)S(1)} collective-permute-done((bf16[7,32,2048]{2,1,0:T(8,128)(2,1)S(1)}, bf16[7,32,2048]{2,1,0:T(8,128)(2,1)S(1)}, u32[]{:S(2)}, u32[]{:S(2)}) %collective-permute-start) | collective-permute-done | bytes 917536 | tf_op jit(solution)/shard_map/ppermute | solution.py:18
  31.4 5.1 %collective-permute-start.1 = (bf16[8,32,2048]{2,1,0:T(8,128)(2,1)}, bf16[8,32,2048]{2,1,0:T(8,128)(2,1)}, u32[]{:S(2)}, u32[]{:S(2)}) collective-permute-start(bf16[8,32,2048]{2,1,0:T(8,128)(2,1)} %get-tuple-element.11), channel_id=1, source_target_pairs={{0,1},{1,2},{2,3},{4,5},{5,6},{6,7},{8,9},{9,10},{10,11},{12,13},{... | collective-permute-start | bytes 3145736 | tf_op jit(solution)/shard_map/ppermute | solution.py:18
  36.5 1.3 slice_select_fusion.1
  37.8 5.3 %fusion.23 = bf16[8,32,2048]{2,1,0:T(8,128)(2,1)} fusion(bf16[16,32,2048]{2,1,0:T(8,128)(2,1)S(1)} %copy-done, bf16[7,32,2048]{2,1,0:T(8,128)(2,1)S(1)} %slice_select_fusion.1, f32[2048]{0:T(1024)S(1)} %bitcast.48, f32[2048]{0:T(1024)S(1)} %bitcast.50, f32[2048]{0:T(1024)S(1)} %bitcast.22, f32[2048]{0:T(1024)S(1)} %bitcast.24, f32[2048]{0:T(1024)S(1)} %bitcast.26, ...), kind=kLoop, calls=%fused_computation.61 | loop fusion | flops 28835840 | bytes 13631488 | tf_op jit(solution)/shard_map/convert_element_type | solution.py:37
  43.1 8.3 %shard_map.52 = (bf16[32,64,256]{2,1,0:T(8,128)(2,1)}, f32[8,1024]{1,0:T(8,128)}) custom-call(bf16[2048,2048]{1,0:T(8,128)(2,1)} %shard_map.50.table, bf16[256,2048]{1,0:T(8,128)(2,1)} %bitcast.19, f32[8,256]{1,0:T(8,128)} %fusion.59.pick), custom_call_target="tpu_custom_call" | custom-call | flops 2147483648 | bytes 8388608 | tf_op jit(solution)/shard_map/pallas_call | solution.py:94
  51.4 5.4 %all-to-all-start.1 = ((bf16[32,64,256]{2,1,0:T(8,128)(2,1)}), bf16[32,64,256]{2,1,0:T(8,128)(2,1)S(1)}, u32[]{:S(2)}, u32[]{:S(2)}) async-start(bf16[32,64,256]{2,1,0:T(8,128)(2,1)} %get-tuple-element.13), calls=%async_computation.1 | async-start | bytes 2097152 | tf_op jit(solution)/shard_map/all_to_all | solution.py:220
  56.9 0.0 collective-permute-done.1
  56.9 1.3 slice_select_fusion
  58.2 5.3 %fusion.24 = bf16[8,32,2048]{2,1,0:T(8,128)(2,1)} fusion(bf16[8,32,2048]{2,1,0:T(8,128)(2,1)S(1)} %slice_select_fusion, bf16[8,32,2048]{2,1,0:T(8,128)(2,1)S(1)} %get-tuple-element.16, bf16[7,32,2048]{2,1,0:T(8,128)(2,1)S(1)} %slice_select_fusion.1, f32[2048]{0:T(1024)S(1)} %bitcast.49, f32[2048]{0:T(1024)S(1)} %bitcast.51, f32[2048]{0:T(1024)S(1)} %bitcast.23, ...), kind=kLoop, calls=%fused_computation.62 | loop fusion | flops 32505856 | bytes 4194304 | tf_op jit(solution)/shard_map/convert_element_type | solution.py:37
  63.6 8.3 %shard_map.51 = (bf16[32,64,256]{2,1,0:T(8,128)(2,1)}, f32[8,1024]{1,0:T(8,128)}) custom-call(bf16[2048,2048]{1,0:T(8,128)(2,1)} %shard_map.50.table, bf16[256,2048]{1,0:T(8,128)(2,1)} %bitcast.18, f32[8,256]{1,0:T(8,128)} %fusion.59.pick), custom_call_target="tpu_custom_call" | custom-call | flops 2147483648 | bytes 8388608 | tf_op jit(solution)/shard_map/pallas_call | solution.py:94
  71.9 0.0 copy-start.4
  71.9 0.0 copy-start.5
  71.9 11.3 %all-to-all-done.1.refs_1_ = bf16[32,64,256]{2,1,0:T(8,128)(2,1)S(1)} async-done(((bf16[32,64,256]{2,1,0:T(8,128)(2,1)}), bf16[32,64,256]{2,1,0:T(8,128)(2,1)S(1)}, u32[]{:S(2)}, u32[]{:S(2)}) %all-to-all-start.1) | async-done | bytes 1048608 | tf_op jit(solution)/shard_map/all_to_all | solution.py:220
  83.2 0.0 copy-start.1
  83.2 4.4 %all-to-all-start = ((bf16[32,64,256]{2,1,0:T(8,128)(2,1)}), bf16[32,64,256]{2,1,0:T(8,128)(2,1)S(1)}, u32[]{:S(2)}, u32[]{:S(2)}) async-start(bf16[32,64,256]{2,1,0:T(8,128)(2,1)} %get-tuple-element.12), calls=%async_computation | async-start | bytes 2097152 | tf_op jit(solution)/shard_map/all_to_all | solution.py:226
  87.6 0.0 reduce-scatter.2.cloned.1.call-start
  87.7 0.0 copy-done.4
  87.7 0.0 copy-done.5
  87.7 0.6 pad_maximum_fusion.3
  88.3 0.0 reduce-scatter.2.cloned.1.call-update
  88.4 35.5 %reduce-scatter.2.cloned.1.call-done = f32[16,128]{1,0:T(8,128)} async-done(((f32[16,1024]{1,0:T(8,128)}), f32[16,128]{1,0:T(8,128)}) %reduce-scatter.2.cloned.1.call-update) | async-done | bytes 8208 | tf_op jit(solution)/shard_map/reduce_scatter | solution.py:229
  123.9 1.3 broadcast_multiply_fusion
  125.2 0.0 all-to-all-done.refs_0_
  125.2 0.0 copy-done.1
  125.2 0.0 copy-start.2
  125.2 1.0 copy-done.2
  126.2 12.5 %shard_map.53 = f32[32,2,256,256]{3,2,1,0:T(8,128)} custom-call(bf16[32,64,256]{2,1,0:T(8,128)(2,1)} %copy-done.2, bf16[32,64,256]{2,1,0:T(8,128)(2,1)} %copy-done.1), custom_call_target="tpu_custom_call" | custom-call | tf_op jit(solution)/shard_map/pallas_call | solution.py:190
  (2 shorter events, 0.0 us)
Async XLA Ops:
  8.4 23.0 %collective-permute-start = (bf16[7,32,2048]{2,1,0:T(8,128)(2,1)S(1)}, bf16[7,32,2048]{2,1,0:T(8,128)(2,1)S(1)}, u32[]{:S(2)}, u32[]{:S(2)}) collective-permute-start(bf16[7,32,2048]{2,1,0:T(8,128)(2,1)S(1)} %slice.182), channel_id=1, source_target_pairs={{0,1},{1,2},{2,3},{4,5},{5,6},{6,7},{8,9},{9,10},{10,11},{12,13},{... | collective-permute-start | bytes 2752520 | tf_op jit(solution)/shard_map/ppermute | solution.py:18
  16.8 6.2 %copy-start.3 = (f32[16,2048]{1,0:T(8,128)S(1)}, f32[16,2048]{1,0:T(8,128)}, u32[]{:S(2)}) copy-start(f32[16,2048]{1,0:T(8,128)} %param.5) | copy-start | bytes 393220
  16.8 6.3 %copy-start = (bf16[16,32,2048]{2,1,0:T(8,128)(2,1)S(1)}, bf16[16,32,2048]{2,1,0:T(8,128)(2,1)}, u32[]{:S(2)}) copy-start(bf16[16,32,2048]{2,1,0:T(8,128)(2,1)} %param.3) | copy-start | bytes 6291460
  31.4 25.4 %collective-permute-start.1 = (bf16[8,32,2048]{2,1,0:T(8,128)(2,1)}, bf16[8,32,2048]{2,1,0:T(8,128)(2,1)}, u32[]{:S(2)}, u32[]{:S(2)}) collective-permute-start(bf16[8,32,2048]{2,1,0:T(8,128)(2,1)} %get-tuple-element.11), channel_id=1, source_target_pairs={{0,1},{1,2},{2,3},{4,5},{5,6},{6,7},{8,9},{9,10},{10,11},{12,13},{... | collective-permute-start | bytes 3145736 | tf_op jit(solution)/shard_map/ppermute | solution.py:18
  51.4 31.8 %all-to-all-start.1 = ((bf16[32,64,256]{2,1,0:T(8,128)(2,1)}), bf16[32,64,256]{2,1,0:T(8,128)(2,1)S(1)}, u32[]{:S(2)}, u32[]{:S(2)}) async-start(bf16[32,64,256]{2,1,0:T(8,128)(2,1)} %get-tuple-element.13), calls=%async_computation.1 | async-start | bytes 2097152 | tf_op jit(solution)/shard_map/all_to_all | solution.py:220
  71.9 15.8 %copy-start.4 = (f32[8,1024]{1,0:T(8,128)S(1)}, f32[8,1024]{1,0:T(8,128)}, u32[]{:S(2)}) copy-start(f32[8,1024]{1,0:T(8,128)} %get-tuple-element.15) | copy-start | bytes 98308
  71.9 15.8 %copy-start.5 = (f32[8,1024]{1,0:T(8,128)S(1)}, f32[8,1024]{1,0:T(8,128)}, u32[]{:S(2)}) copy-start(f32[8,1024]{1,0:T(8,128)} %get-tuple-element.14) | copy-start | bytes 98308
  83.2 41.9 %copy-start.1 = (bf16[32,64,256]{2,1,0:T(8,128)(2,1)}, bf16[32,64,256]{2,1,0:T(8,128)(2,1)S(1)}, u32[]{:S(2)}) copy-start(bf16[32,64,256]{2,1,0:T(8,128)(2,1)S(1)} %all-to-all-done.1.refs_1_) | copy-start | bytes 3145732
  83.2 41.9 %all-to-all-start = ((bf16[32,64,256]{2,1,0:T(8,128)(2,1)}), bf16[32,64,256]{2,1,0:T(8,128)(2,1)S(1)}, u32[]{:S(2)}, u32[]{:S(2)}) async-start(bf16[32,64,256]{2,1,0:T(8,128)(2,1)} %get-tuple-element.12), calls=%async_computation | async-start | bytes 2097152 | tf_op jit(solution)/shard_map/all_to_all | solution.py:226
  87.6 36.2 %reduce-scatter.2.cloned.1.call-start = ((), (), s32[]{:S(2)}) async-start(), calls=%async_computation.3 | async-start | bytes 73728 | tf_op jit(solution)/shard_map/reduce_scatter | solution.py:229
  125.2 1.0 copy-start.2
Sparse Core Ops, SparseCore 0:
  92.0 31.7 reduce-scatter.1

commit v3 on v2

--- a/solution.py
+++ b/solution.py
@@ -9,7 +9,7 @@
 from jax.sharding import PartitionSpec as P
 
 BOTH = ("station", "tm")
-VMEM_LIMIT = 56 * 1024 * 1024
+VMEM_LIMIT = 24 * 1024 * 1024
 
 
 def passed_along(block, axis, distance):
@@ -150,52 +150,99 @@
     return flat, turned
 
 
-def correlate_kernel(stations, blocks, own, local, scale, *refs):
-    *parts, vis, wide = refs
-    chunks = parts[0].shape[2] // 128
+def spread(got, wide, stations, blocks, own):
+    chunks = got.shape[2] // 128
+
+    def fill(s, carry):
+        for tm in range(blocks):
+            for p in range(2):
+                piece = got[s * blocks + tm, p * own : (p + 1) * own, :].astype(jnp.float32)
+                base = (p * blocks + tm) * own
+                for j in range(chunks):
+                    wide[s * chunks + j, base : base + own, :] = piece[:, j * 128 : (j + 1) * 128]
+        return carry
+
+    lax.fori_loop(0, stations, fill, 0)
+
+
+def arrange_kernel(stations, blocks, own, local, got, both, wide):
+    step = pl.program_id(0)
+    group = both.shape[0]
+    pl.when(step == 0)(lambda: spread(got, wide, stations, blocks, own))
+    for g in range(group):
+        pair = channel_rows(wide, step * group + g, stations, blocks, own, local)
+        both[g] = jnp.concatenate(pair, axis=1)
+
+
+def correlate_kernel(stations, blocks, own, local, scale, got, late, vis, wide):
+    step = pl.program_id(0)
     group = vis.shape[0]
     inputs = stations * local
-    step = pl.program_id(0)
-
-    @pl.when(step == 0)
-    def _():
-        def fill(s, carry):
-            for i, got in enumerate(parts):
-                for tm in range(blocks):
-                    for p in range(2):
-                        piece = got[s * blocks + tm, p * own : (p + 1) * own, :]
-                        piece = piece.astype(jnp.float32)
-                        base = (p * blocks + tm) * own
-                        for j in range(chunks):
-                            at = (s * len(parts) + i) * chunks + j
-                            wide[at, base : base + own, :] = piece[:, j * 128 : (j + 1) * 128]
-            return carry
-
-        lax.fori_loop(0, stations, fill, 0)
-
+    pl.when(step == 0)(lambda: spread(got, wide, stations, blocks, own))
     for g in range(group):
-        flat, turned = channel_rows(wide, step * group + g, stations, blocks, own, local)
-        both = jnp.concatenate([flat, turned], axis=1)
+        pair = channel_rows(wide, step * group + g, stations, blocks, own, local)
+        both = jnp.concatenate([jnp.concatenate(pair, axis=1), late[g]], axis=0)
         out = lax.dot_general(
-            flat, both, (((0,), (0,)), ((), ())), preferred_element_type=jnp.float32
+            both[:, :inputs],
+            both,
+            (((0,), (0,)), ((), ())),
+            preferred_element_type=jnp.float32,
         )
         vis[g, 0] = out[:, :inputs] * scale
         vis[g, 1] = out[:, inputs:] * scale
 
 
-def correlate(parts, stations, blocks, own, local, scale):
+def arrange(got, stations, blocks, own, local):
     inputs = stations * local
-    chunks = sum(got.shape[2] for got in parts) // 128
+    depth = got.shape[2] // local * blocks * 2
+    group = math.gcd(own, 4)
+    return pl.pallas_call(
+        functools.partial(arrange_kernel, stations, blocks, own, local),
+        grid=(own // group,),
+        in_specs=[pl.BlockSpec(memory_space=pltpu.VMEM)],
+        out_specs=pl.BlockSpec((group, depth, 2 * inputs), lambda c: (c, 0, 0)),
+        out_shape=jax.ShapeDtypeStruct((own, depth, 2 * inputs), jnp.bfloat16),
+        scratch_shapes=[
+            pltpu.VMEM((stations * got.shape[2] // 128, 2 * blocks * own, 128), jnp.float32)
+        ],
+        compiler_params=pltpu.CompilerParams(vmem_limit_bytes=VMEM_LIMIT),
+        cost_estimate=pl.CostEstimate(
+            flops=got.size * 100, bytes_accessed=got.size * 12, transcendentals=0
+        ),
+    )(got)
+
+
+def correlate(got, late, stations, blocks, own, local, scale):
+    inputs = stations * local
     group = math.gcd(own, 4)
     return pl.pallas_call(
         functools.partial(correlate_kernel, stations, blocks, own, local, scale),
         grid=(own // group,),
-        in_specs=[pl.BlockSpec(got.shape, lambda c: (0, 0, 0)) for got in parts],
+        in_specs=[
+            pl.BlockSpec(memory_space=pltpu.VMEM),
+            pl.BlockSpec((group,) + late.shape[1:], lambda c: (c, 0, 0)),
+        ],
         out_specs=pl.BlockSpec((group, 2, inputs, inputs), lambda c: (c, 0, 0, 0)),
         out_shape=jax.ShapeDtypeStruct((own, 2, inputs, inputs), jnp.float32),
-        scratch_shapes=[pltpu.VMEM((stations * chunks, 2 * blocks * own, 128), jnp.float32)],
-        compiler_params=pltpu.CompilerParams(vmem_limit_bytes=VMEM_LIMIT),
-    )(*parts)
+        scratch_shapes=[
+            pltpu.VMEM((stations * got.shape[2] // 128, 2 * blocks * own, 128), jnp.float32)
+        ],
+        compiler_params=pltpu.CompilerParams(vmem_limit_bytes=VMEM_LIMIT),
+    )(got, late)
+
+
+def sum_scatter(rows):
+    count = rows.shape[0]
+    me = lax.axis_index("station")
+    distance = count // 2
+    while distance > 0:
+        upper = me // distance % 2 == 1
+        low, high = rows[:distance], rows[distance:]
+        route = [(i, i ^ distance) for i in range(count)]
+        other = lax.ppermute(jnp.where(upper, low, high), "station", route)
+        rows = jnp.where(upper, high, low) + other
+        distance //= 2
+    return rows[0]
 
 
 def body(samples, history, taps):
@@ -223,13 +270,17 @@
     early = filter_frames(jnp.concatenate([far, near, samples[:half]], axis=0), taps, half)
     early = early.reshape(half * local, frame_len)
     spec_early, power_early = channelise(table, early, own, half, dests, group)
+    got_late, spec_early, power_early = lax.optimization_barrier(
+        (got_late, spec_early, power_early)
+    )
     got_early = lax.all_to_all(spec_early, BOTH, split_axis=0, concat_axis=0, tiled=True)
 
     power = jnp.concatenate([power_early, power_late], axis=0)
-    power = lax.psum_scatter(power, "station", scatter_dimension=1, tiled=True)
+    power = sum_scatter(power.reshape(frames_dev, stations, blocks * own).transpose(1, 0, 2))
     power = power * (1.0 / (stations * local))
     scale = 1.0 / (frames_dev * blocks)
-    visibility = correlate((got_early, got_late), stations, blocks, own, local, scale)
+    arranged = arrange(got_late, stations, blocks, own, local)
+    visibility = correlate(got_early, arranged, stations, blocks, own, local, scale)
     return visibility, power
 
 

time: 147 us -> 119 us (0.81)
  waiting for transfers between devices: 53.9 us -> 37.4 us
  between operations: 14.1 us -> 0.86 us
  starting transfers between devices: 19 us -> 31.4 us
  Pallas kernels: 35.3 us -> 27.7 us
  other arithmetic: 19.5 us -> 14.5 us
  local copies, waits for them, and re-layouts: 3.6 us -> 6.22 us
    reduce_scatter x1 -> x0, waiting for transfers between devices: 35.5 us -> none  [body(): power = lax.psum_scatter(power, 'station', scatter_dimension=1, tiled=True)]
    ppermute x0 -> x3, starting transfers between devices: none -> 9.13 us  [sum_scatter(): other = lax.ppermute(jnp.where(upper, low, high), 'station', route)]
    ppermute x2, waiting for transfers between devices: 7.04 us -> 15.5 us  [passed_along(): return lax.ppermute(block, axis, route)]
    all_to_all x1, waiting for transfers between devices: 0.01 us -> 8.07 us  [body(): lax.all_to_all(spec_early, BOTH, split_axis=0, concat_axis=0, tiled=True)]
    ppermute x0 -> x3, waiting for transfers between devices: none -> 5.71 us  [sum_scatter(): other = lax.ppermute(jnp.where(upper, low, high), 'station', route)]
    pallas_call x2, Pallas kernels: 16.7 us -> 11.7 us  [channelise(): pl.pallas_call(functools.partial(dft_kernel, own), grid=(dests // group,)...]
    pallas_call x1, Pallas kernels: 6.2 us -> 2.67 us  [dft_table(): pl.pallas_call(functools.partial(table_kernel, own), grid=(dests // group...]
    all_to_all x1, starting transfers between devices: 4.38 us -> 7.62 us  [body(): lax.all_to_all(spec_early, BOTH, split_axis=0, concat_axis=0, tiled=True)]
  transfers between devices with their start and end apart: 5 -> 7, of which waited for: 3 -> 6; matrix products, arithmetic and copies ran while one was open for 14% -> 14% of each run, Pallas kernels for 16% -> 15%
where the time goes in v3:
time: 119 us; the launch traced here: 118 us
  waiting for transfers between devices  37.4 us (31%)
  starting transfers between devices  31.4 us (26%)
  Pallas kernels  27.7 us (23%)
  other arithmetic  14.5 us (12%)
  local copies, waits for them, and re-layouts  6.22 us (5%)
    ppermute x2, waiting for transfers between devices, passed_along(): return lax.ppermute(block, axis, route)  15.5 us
    pallas_call x2, Pallas kernels, channelise(): pl.pallas_call(functools.partial(dft_kernel, own), grid=(dests // group,)...  11.7 us
    pallas_call x1, Pallas kernels, correlate(): pl.pallas_call(functools.partial(correlate_kernel, stations, blocks, own,...  10.5 us
    ppermute x2, starting transfers between devices, passed_along(): return lax.ppermute(block, axis, route)  9.19 us
    ppermute x3, starting transfers between devices, sum_scatter(): other = lax.ppermute(jnp.where(upper, low, high), 'station', route)  9.13 us
    convert_element_type x2, other arithmetic, filter_frames(): return running.astype(jnp.bfloat16)  9.11 us
    all_to_all x1, waiting for transfers between devices, body(): lax.all_to_all(spec_late, BOTH, split_axis=0, concat_axis=0, tiled=True)  8.11 us
    all_to_all x1, waiting for transfers between devices, body(): lax.all_to_all(spec_early, BOTH, split_axis=0, concat_axis=0, tiled=True)  8.07 us
  transfers between devices with their start and end apart: 7, of which 6 were waited for; matrix products, arithmetic and copies ran while one was open for 14% of the time, Pallas kernels for 15%

profile of v3, /device:TPU:1, one launch (start us, length us, event | category | flops | bytes accessed | tf_op | source)
XLA Modules:
  0.0 118.0 jit_solution(17040114789421375709)
XLA Ops:
  0.6 1.2 %slice.200 = bf16[7,32,2048]{2,1,0:T(8,128)(2,1)S(1)} slice(bf16[16,32,2048]{2,1,0:T(8,128)(2,1)} %param.3), slice={[9:16], [0:32], [0:2048]} | slice | bytes 1835008 | tf_op jit(solution)/shard_map/slice | solution.py:259
  1.9 4.1 %collective-permute-start = (bf16[7,32,2048]{2,1,0:T(8,128)(2,1)S(1)}, bf16[7,32,2048]{2,1,0:T(8,128)(2,1)S(1)}, u32[]{:S(2)}, u32[]{:S(2)}) collective-permute-start(bf16[7,32,2048]{2,1,0:T(8,128)(2,1)S(1)} %slice.200), channel_id=1, source_target_pairs={{0,1},{1,2},{2,3},{4,5},{5,6},{6,7},{8,9},{9,10},{10,11},{12,13},{... | collective-permute-start | bytes 2752520 | tf_op jit(solution)/shard_map/ppermute | solution.py:18
  6.0 1.0 fusion.55
  7.0 1.1 fusion.57
  8.1 0.0 copy-start.3
  8.2 0.0 copy-start.2
  8.2 2.7 %shard_map.50.table = bf16[2048,2048]{1,0:T(8,128)(2,1)S(1)} custom-call(f32[32,2048]{1,0:T(8,128)S(1)} %get-tuple-element.41.cos_hi, f32[32,2048]{1,0:T(8,128)S(1)} %get-tuple-element.40.sin_hi, f32[32,2048]{1,0:T(8,128)S(1)} %get-tuple-element.43.cos_lo, f32[32,2048]{1,0:T(8,128)S(1)} %get-tuple-element.42.sin_lo), custom_call_target="tpu_custom_call" | custom-call | flops 16777216 | bytes 8388608 | tf_op jit(solution)/shard_map/pallas_call | solution.py:56
  10.8 0.0 copy-done.3
  10.9 0.0 copy-start
  10.9 0.1 fusion.61
  11.0 0.0 copy-done.2
  11.0 1.5 %fusion.60 = (bf16[8,32,2048]{2,1,0:T(8,128)(2,1)S(1)}, bf16[8,32,2048]{2,1,0:T(8,128)(2,1)}) fusion(bf16[16,32,2048]{2,1,0:T(8,128)(2,1)S(1)} %copy-done.2), kind=kLoop, calls=%fused_computation.123 | loop fusion | bytes 4194304 | tf_op jit(solution)/shard_map/slice | solution.py:34
  12.5 12.4 %collective-permute-done = bf16[7,32,2048]{2,1,0:T(8,128)(2,1)S(1)} collective-permute-done((bf16[7,32,2048]{2,1,0:T(8,128)(2,1)S(1)}, bf16[7,32,2048]{2,1,0:T(8,128)(2,1)S(1)}, u32[]{:S(2)}, u32[]{:S(2)}) %collective-permute-start) | collective-permute-done | bytes 917536 | tf_op jit(solution)/shard_map/ppermute | solution.py:18
  24.9 5.1 %collective-permute-start.1 = (bf16[8,32,2048]{2,1,0:T(8,128)(2,1)}, bf16[8,32,2048]{2,1,0:T(8,128)(2,1)}, u32[]{:S(2)}, u32[]{:S(2)}) collective-permute-start(bf16[8,32,2048]{2,1,0:T(8,128)(2,1)} %get-tuple-element.15), channel_id=1, source_target_pairs={{0,1},{1,2},{2,3},{4,5},{5,6},{6,7},{8,9},{9,10},{10,11},{12,13},{... | collective-permute-start | bytes 3145736 | tf_op jit(solution)/shard_map/ppermute | solution.py:18
  30.0 1.3 %slice_select_fusion.1 = bf16[7,32,2048]{2,1,0:T(8,128)(2,1)S(1)} fusion(bf16[7,32,2048]{2,1,0:T(8,128)(2,1)S(1)} %collective-permute-done, bf16[15,32,2048]{2,1,0:T(8,128)(2,1)} %param.4, pred[]{:T(512)S(6)} %eq.45), kind=kLoop, calls=%fused_computation.85 | loop fusion | flops 458752 | bytes 2752513 | tf_op jit(solution)/shard_map/jit(_where)/select_n | solution.py:263
  31.3 4.5 %fusion.8 = bf16[8,32,2048]{2,1,0:T(8,128)(2,1)S(1)} fusion(bf16[16,32,2048]{2,1,0:T(8,128)(2,1)S(1)} %copy-done.2, bf16[7,32,2048]{2,1,0:T(8,128)(2,1)S(1)} %slice_select_fusion.1, f32[2048]{0:T(1024)S(1)} %bitcast.57, f32[2048]{0:T(1024)S(1)} %bitcast.59, f32[2048]{0:T(1024)S(1)} %bitcast.31, f32[2048]{0:T(1024)S(1)} %bitcast.33, f32[2048]{0:T(1024)S(1)} %bitcast.35, ...), kind=kLoop, calls=%fused_computation.46 | loop fusion | flops 28835840 | bytes 13631488 | tf_op jit(solution)/shard_map/convert_element_type | solution.py:37
  35.8 0.0 copy-done
  35.9 5.9 %shard_map.51 = (bf16[32,64,256]{2,1,0:T(8,128)(2,1)}, f32[8,1024]{1,0:T(8,128)S(1)}) custom-call(bf16[2048,2048]{1,0:T(8,128)(2,1)S(1)} %shard_map.50.table, bf16[256,2048]{1,0:T(8,128)(2,1)S(1)} %bitcast.28, f32[8,256]{1,0:T(8,128)S(1)} %fusion.59.pick), custom_call_target="tpu_custom_call" | custom-call | flops 2147483648 | bytes 8388608 | tf_op jit(solution)/shard_map/pallas_call | solution.py:94
  41.7 5.4 %all-to-all-start = ((bf16[32,64,256]{2,1,0:T(8,128)(2,1)}), bf16[32,64,256]{2,1,0:T(8,128)(2,1)S(1)}, u32[]{:S(2)}, u32[]{:S(2)}) async-start(bf16[32,64,256]{2,1,0:T(8,128)(2,1)} %get-tuple-element.14), calls=%async_computation | async-start | bytes 2097152 | tf_op jit(solution)/shard_map/all_to_all | solution.py:267
  47.2 3.1 %collective-permute-done.1 = bf16[8,32,2048]{2,1,0:T(8,128)(2,1)} collective-permute-done((bf16[8,32,2048]{2,1,0:T(8,128)(2,1)}, bf16[8,32,2048]{2,1,0:T(8,128)(2,1)}, u32[]{:S(2)}, u32[]{:S(2)}) %collective-permute-start.1) | collective-permute-done | bytes 1048608 | tf_op jit(solution)/shard_map/ppermute | solution.py:18
  50.2 1.3 %slice_select_fusion = bf16[8,32,2048]{2,1,0:T(8,128)(2,1)S(1)} fusion(bf16[8,32,2048]{2,1,0:T(8,128)(2,1)} %collective-permute-done.1, bf16[15,32,2048]{2,1,0:T(8,128)(2,1)} %param.4, pred[]{:T(512)S(6)} %eq.45), kind=kLoop, calls=%fused_computation.84 | loop fusion | flops 524288 | bytes 3145729 | tf_op jit(solution)/shard_map/jit(_where)/select_n | solution.py:269
  51.6 4.6 %fusion.24 = bf16[8,32,2048]{2,1,0:T(8,128)(2,1)S(1)} fusion(bf16[8,32,2048]{2,1,0:T(8,128)(2,1)S(1)} %slice_select_fusion, bf16[8,32,2048]{2,1,0:T(8,128)(2,1)S(1)} %get-tuple-element.22, bf16[7,32,2048]{2,1,0:T(8,128)(2,1)S(1)} %slice_select_fusion.1, f32[2048]{0:T(1024)S(1)} %bitcast.58, f32[2048]{0:T(1024)S(1)} %bitcast.60, f32[2048]{0:T(1024)S(1)} %bitcast.32, ...), kind=kLoop, calls=%fused_computation.62 | loop fusion | flops 32505856 | bytes 4194304 | tf_op jit(solution)/shard_map/convert_element_type | solution.py:37
  56.2 0.0 copy-start.1
  56.2 3.4 %copy-done.1 = bf16[2048,2048]{1,0:T(8,128)(2,1)S(1)} copy-done((bf16[2048,2048]{1,0:T(8,128)(2,1)S(1)}, bf16[2048,2048]{1,0:T(8,128)(2,1)}, u32[]{:S(2)}) %copy-start.1) | copy-done | bytes 8388632
  59.5 5.9 %shard_map.52 = (bf16[32,64,256]{2,1,0:T(8,128)(2,1)}, f32[8,1024]{1,0:T(8,128)S(1)}) custom-call(bf16[2048,2048]{1,0:T(8,128)(2,1)S(1)} %copy-done.1, bf16[256,2048]{1,0:T(8,128)(2,1)S(1)} %bitcast.27, f32[8,256]{1,0:T(8,128)S(1)} %fusion.59.pick), custom_call_target="tpu_custom_call" | custom-call | flops 2147483648 | bytes 8388608 | tf_op jit(solution)/shard_map/pallas_call | solution.py:94
  65.4 8.1 %all-to-all-done.got = bf16[32,64,256]{2,1,0:T(8,128)(2,1)S(1)} async-done(((bf16[32,64,256]{2,1,0:T(8,128)(2,1)}), bf16[32,64,256]{2,1,0:T(8,128)(2,1)S(1)}, u32[]{:S(2)}, u32[]{:S(2)}) %all-to-all-start) | async-done | bytes 1048608 | tf_op jit(solution)/shard_map/all_to_all | solution.py:267
  73.5 7.6 %all-to-all-start.1 = ((bf16[32,64,256]{2,1,0:T(8,128)(2,1)}), bf16[32,64,256]{2,1,0:T(8,128)(2,1)}, u32[]{:S(2)}, u32[]{:S(2)}) async-start(bf16[32,64,256]{2,1,0:T(8,128)(2,1)} %get-tuple-element.18), calls=%async_computation.1 | async-start | bytes 2097152 | tf_op jit(solution)/shard_map/all_to_all | solution.py:276
  81.2 1.5 %collective-permute-start.2 = (f32[4,16,128]{2,1,0:T(8,128)S(1)}, f32[4,16,128]{2,1,0:T(8,128)S(1)}, u32[]{:S(2)}, u32[]{:S(2)}) collective-permute-start(f32[4,16,128]{2,1,0:T(8,128)S(1)} %slice_select_fusion.2), channel_id=1, source_target_pairs={{0,16},{4,20},{8,24},{12,28},{16,0},{20,4},{24,8},{28,12},{1,17},{... | collective-permute-start | bytes 98312 | tf_op jit(solution)/shard_map/ppermute | solution.py:242
  82.7 4.2 %collective-permute-done.2 = f32[4,16,128]{2,1,0:T(8,128)S(1)} collective-permute-done((f32[4,16,128]{2,1,0:T(8,128)S(1)}, f32[4,16,128]{2,1,0:T(8,128)S(1)}, u32[]{:S(2)}, u32[]{:S(2)}) %collective-permute-start.2) | collective-permute-done | bytes 32800 | tf_op jit(solution)/shard_map/ppermute | solution.py:242
  86.9 3.0 %collective-permute-start.3 = (f32[2,16,128]{2,1,0:T(8,128)S(1)}, f32[2,16,128]{2,1,0:T(8,128)S(1)}, u32[]{:S(2)}, u32[]{:S(2)}) collective-permute-start(f32[2,16,128]{2,1,0:T(8,128)S(1)} %slice_select_fusion.3), channel_id=1, source_target_pairs={{0,8},{4,12},{8,0},{12,4},{16,24},{20,28},{24,16},{28,20},{1,9},{5... | collective-permute-start | bytes 49160 | tf_op jit(solution)/shard_map/ppermute | solution.py:242
  89.8 1.5 %collective-permute-done.3 = f32[2,16,128]{2,1,0:T(8,128)S(1)} collective-permute-done((f32[2,16,128]{2,1,0:T(8,128)S(1)}, f32[2,16,128]{2,1,0:T(8,128)S(1)}, u32[]{:S(2)}, u32[]{:S(2)}) %collective-permute-start.3) | collective-permute-done | bytes 16416 | tf_op jit(solution)/shard_map/ppermute | solution.py:242
  91.4 4.7 %collective-permute-start.4 = (f32[1,16,128]{2,1,0:T(8,128)S(1)}, f32[1,16,128]{2,1,0:T(8,128)S(1)}, u32[]{:S(2)}, u32[]{:S(2)}) collective-permute-start(f32[1,16,128]{2,1,0:T(8,128)S(1)} %slice_select_fusion.4), channel_id=1, source_target_pairs={{0,4},{4,0},{8,12},{12,8},{16,20},{20,16},{24,28},{28,24},{1,5},{5... | collective-permute-start | bytes 24584 | tf_op jit(solution)/shard_map/ppermute | solution.py:242
  96.1 2.8 %shard_map.53.late = bf16[32,64,512]{2,1,0:T(8,128)(2,1)S(1)} custom-call(bf16[32,64,256]{2,1,0:T(8,128)(2,1)S(1)} %all-to-all-done.got), custom_call_target="tpu_custom_call" | custom-call | flops 52428800 | bytes 6291456 | tf_op jit(solution)/shard_map/pallas_call | solution.py:199
  98.9 0.0 collective-permute-done.4
  98.9 0.6 multiply_bitcast_fusion
  99.5 8.1 %all-to-all-done.1.got = bf16[32,64,256]{2,1,0:T(8,128)(2,1)} async-done(((bf16[32,64,256]{2,1,0:T(8,128)(2,1)}), bf16[32,64,256]{2,1,0:T(8,128)(2,1)}, u32[]{:S(2)}, u32[]{:S(2)}) %all-to-all-start.1) | async-done | bytes 1048608 | tf_op jit(solution)/shard_map/all_to_all | solution.py:276
  107.5 10.5 %shard_map.54 = f32[32,2,256,256]{3,2,1,0:T(8,128)} custom-call(bf16[32,64,256]{2,1,0:T(8,128)(2,1)} %all-to-all-done.1.got, bf16[32,64,512]{2,1,0:T(8,128)(2,1)S(1)} %shard_map.53.late), custom_call_target="tpu_custom_call" | custom-call | tf_op jit(solution)/shard_map/pallas_call | solution.py:218
  (9 shorter events, 0.1 us)
Async XLA Ops:
  1.9 23.0 %collective-permute-start = (bf16[7,32,2048]{2,1,0:T(8,128)(2,1)S(1)}, bf16[7,32,2048]{2,1,0:T(8,128)(2,1)S(1)}, u32[]{:S(2)}, u32[]{:S(2)}) collective-permute-start(bf16[7,32,2048]{2,1,0:T(8,128)(2,1)S(1)} %slice.200), channel_id=1, source_target_pairs={{0,1},{1,2},{2,3},{4,5},{5,6},{6,7},{8,9},{9,10},{10,11},{12,13},{... | collective-permute-start | bytes 2752520 | tf_op jit(solution)/shard_map/ppermute | solution.py:18
  8.1 2.7 %copy-start.3 = (f32[16,2048]{1,0:T(8,128)S(1)}, f32[16,2048]{1,0:T(8,128)}, u32[]{:S(2)}) copy-start(f32[16,2048]{1,0:T(8,128)} %param.5) | copy-start | bytes 393220
  8.2 2.8 %copy-start.2 = (bf16[16,32,2048]{2,1,0:T(8,128)(2,1)S(1)}, bf16[16,32,2048]{2,1,0:T(8,128)(2,1)}, u32[]{:S(2)}) copy-start(bf16[16,32,2048]{2,1,0:T(8,128)(2,1)} %param.3) | copy-start | bytes 6291460
  10.9 25.0 %copy-start = (bf16[2048,2048]{1,0:T(8,128)(2,1)}, bf16[2048,2048]{1,0:T(8,128)(2,1)S(1)}, u32[]{:S(2)}) copy-start(bf16[2048,2048]{1,0:T(8,128)(2,1)S(1)} %shard_map.50.table) | copy-start | bytes 25165828
  24.9 25.3 %collective-permute-start.1 = (bf16[8,32,2048]{2,1,0:T(8,128)(2,1)}, bf16[8,32,2048]{2,1,0:T(8,128)(2,1)}, u32[]{:S(2)}, u32[]{:S(2)}) collective-permute-start(bf16[8,32,2048]{2,1,0:T(8,128)(2,1)} %get-tuple-element.15), channel_id=1, source_target_pairs={{0,1},{1,2},{2,3},{4,5},{5,6},{6,7},{8,9},{9,10},{10,11},{12,13},{... | collective-permute-start | bytes 3145736 | tf_op jit(solution)/shard_map/ppermute | solution.py:18
  41.7 31.8 %all-to-all-start = ((bf16[32,64,256]{2,1,0:T(8,128)(2,1)}), bf16[32,64,256]{2,1,0:T(8,128)(2,1)S(1)}, u32[]{:S(2)}, u32[]{:S(2)}) async-start(bf16[32,64,256]{2,1,0:T(8,128)(2,1)} %get-tuple-element.14), calls=%async_computation | async-start | bytes 2097152 | tf_op jit(solution)/shard_map/all_to_all | solution.py:267
  56.2 3.4 %copy-start.1 = (bf16[2048,2048]{1,0:T(8,128)(2,1)S(1)}, bf16[2048,2048]{1,0:T(8,128)(2,1)}, u32[]{:S(2)}) copy-start(bf16[2048,2048]{1,0:T(8,128)(2,1)} %copy-done) | copy-start | bytes 25165828
  73.5 34.0 %all-to-all-start.1 = ((bf16[32,64,256]{2,1,0:T(8,128)(2,1)}), bf16[32,64,256]{2,1,0:T(8,128)(2,1)}, u32[]{:S(2)}, u32[]{:S(2)}) async-start(bf16[32,64,256]{2,1,0:T(8,128)(2,1)} %get-tuple-element.18), calls=%async_computation.1 | async-start | bytes 2097152 | tf_op jit(solution)/shard_map/all_to_all | solution.py:276
  81.2 5.6 %collective-permute-start.2 = (f32[4,16,128]{2,1,0:T(8,128)S(1)}, f32[4,16,128]{2,1,0:T(8,128)S(1)}, u32[]{:S(2)}, u32[]{:S(2)}) collective-permute-start(f32[4,16,128]{2,1,0:T(8,128)S(1)} %slice_select_fusion.2), channel_id=1, source_target_pairs={{0,16},{4,20},{8,24},{12,28},{16,0},{20,4},{24,8},{28,12},{1,17},{... | collective-permute-start | bytes 98312 | tf_op jit(solution)/shard_map/ppermute | solution.py:242
  86.9 4.5 %collective-permute-start.3 = (f32[2,16,128]{2,1,0:T(8,128)S(1)}, f32[2,16,128]{2,1,0:T(8,128)S(1)}, u32[]{:S(2)}, u32[]{:S(2)}) collective-permute-start(f32[2,16,128]{2,1,0:T(8,128)S(1)} %slice_select_fusion.3), channel_id=1, source_target_pairs={{0,8},{4,12},{8,0},{12,4},{16,24},{20,28},{24,16},{28,20},{1,9},{5... | collective-permute-start | bytes 49160 | tf_op jit(solution)/shard_map/ppermute | solution.py:242
  91.4 7.5 %collective-permute-start.4 = (f32[1,16,128]{2,1,0:T(8,128)S(1)}, f32[1,16,128]{2,1,0:T(8,128)S(1)}, u32[]{:S(2)}, u32[]{:S(2)}) collective-permute-start(f32[1,16,128]{2,1,0:T(8,128)S(1)} %slice_select_fusion.4), channel_id=1, source_target_pairs={{0,4},{4,0},{8,12},{12,8},{16,20},{20,16},{24,28},{28,24},{1,5},{5... | collective-permute-start | bytes 24584 | tf_op jit(solution)/shard_map/ppermute | solution.py:242

commit v4 on v3

--- a/solution.py
+++ b/solution.py
@@ -9,7 +9,7 @@
 from jax.sharding import PartitionSpec as P
 
 BOTH = ("station", "tm")
-VMEM_LIMIT = 24 * 1024 * 1024
+VMEM_LIMIT = 14 * 1024 * 1024
 
 
 def passed_along(block, axis, distance):
@@ -26,15 +26,19 @@
     return jnp.cos(angles), jnp.sin(angles)
 
 
-def filter_frames(extended, taps, frames_out):
+def filter_frames(extended, taps, frames_out, first_tap=0):
     span_taps = taps.shape[0]
     running = jnp.zeros((frames_out,) + extended.shape[1:], jnp.float32)
-    for tap_index in range(span_taps):
+    for tap_index in range(first_tap, span_taps):
         offset = span_taps - 1 - tap_index
         running = running + taps[tap_index][None, None, :] * extended[
             offset : offset + frames_out
         ].astype(jnp.float32)
-    return running.astype(jnp.bfloat16)
+    return running
+
+
+def padded(frames, before, after):
+    return jnp.pad(frames, ((before, after), (0, 0), (0, 0)))
 
 
 def table_kernel(own, cos_hi, sin_hi, cos_lo, sin_lo, table):
@@ -48,9 +52,7 @@
         )
 
 
-def dft_table(own, dests, group, frame_len):
-    cos_hi, sin_hi = angle_tables(dests, own, frame_len)
-    cos_lo, sin_lo = angle_tables(own, 1, frame_len)
+def dft_table(angles, own, dests, group, frame_len):
     high = pl.BlockSpec((group, frame_len), lambda i: (i, 0))
     low = pl.BlockSpec((own, frame_len), lambda i: (0, 0))
     return pl.pallas_call(
@@ -65,7 +67,7 @@
             bytes_accessed=dests * own * frame_len * 4,
             transcendentals=0,
         ),
-    )(cos_hi, sin_hi, cos_lo, sin_lo)
+    )(*angles)
 
 
 def dft_kernel(own, table, weighted, pick, spec, power):
@@ -87,7 +89,7 @@
     )
 
 
-def channelise(table, weighted, own, frames, dests, group):
+def channelise(table, weighted, own, frames, dests, group, limit):
     rows, frame_len = weighted.shape
     column = jnp.arange(rows, dtype=jnp.int32) // (rows // frames)
     pick = (column[None, :] == jnp.arange(frames, dtype=jnp.int32)[:, None]).astype(jnp.float32)
@@ -107,7 +109,7 @@
             jax.ShapeDtypeStruct((dests, 2 * own, rows), jnp.bfloat16),
             jax.ShapeDtypeStruct((frames, dests * own), jnp.float32),
         ],
-        compiler_params=pltpu.CompilerParams(vmem_limit_bytes=VMEM_LIMIT),
+        compiler_params=pltpu.CompilerParams(vmem_limit_bytes=limit),
         cost_estimate=pl.CostEstimate(
             flops=4 * dests * own * frame_len * rows,
             bytes_accessed=dests * own * frame_len * 4,
@@ -214,7 +216,7 @@
 
 def correlate(got, late, stations, blocks, own, local, scale):
     inputs = stations * local
-    group = math.gcd(own, 4)
+    group = math.gcd(own, 2)
     return pl.pallas_call(
         functools.partial(correlate_kernel, stations, blocks, own, local, scale),
         grid=(own // group,),
@@ -257,19 +259,34 @@
     tail = samples[frames_dev - span :]
 
     near = passed_along(tail[half:], "tm", 1)
-    table = dft_table(own, dests, group, frame_len)
-    near, far_tail, table = lax.optimization_barrier((near, tail[:half], table))
+    angles = angle_tables(dests, own, frame_len) + angle_tables(own, 1, frame_len)
+    table = dft_table(angles, own, dests, group, frame_len)
+    own_late = filter_frames(padded(samples, span - half, 0), taps, half)
+    near, far_tail, table, own_late = lax.optimization_barrier(
+        (near, tail[:half], table, own_late)
+    )
     far = passed_along(far_tail, "tm", 1)
     near = jnp.where(first, history[half:], near)
-    late = filter_frames(jnp.concatenate([near, samples], axis=0), taps, half)
-    late = late.reshape(half * local, frame_len)
-    spec_late, power_late = channelise(table, late, own, half, dests, group)
+    late = own_late + filter_frames(padded(near, 0, half), taps, half, half + 1)
+    late = late.astype(jnp.bfloat16).reshape(half * local, frame_len)
+    own_early = filter_frames(
+        padded(jnp.concatenate([near, samples[:half]], axis=0), half, 0), taps, half
+    )
+    late, own_early = lax.optimization_barrier((late, own_early))
+    spec_late, power_late = channelise(
+        table, late, own, half, dests, group, VMEM_LIMIT
+    )
     got_late = lax.all_to_all(spec_late, BOTH, split_axis=0, concat_axis=0, tiled=True)
 
+    far, spec_late, power_late = lax.optimization_barrier((far, spec_late, power_late))
     far = jnp.where(first, history[:half], far)
-    early = filter_frames(jnp.concatenate([far, near, samples[:half]], axis=0), taps, half)
-    early = early.reshape(half * local, frame_len)
-    spec_early, power_early = channelise(table, early, own, half, dests, group)
+    early = own_early + filter_frames(
+        padded(far, 0, span - half), taps, half, span - half + 1
+    )
+    early = early.astype(jnp.bfloat16).reshape(half * local, frame_len)
+    spec_early, power_early = channelise(
+        table, early, own, half, dests, group, 4 * VMEM_LIMIT
+    )
     got_late, spec_early, power_early = lax.optimization_barrier(
         (got_late, spec_early, power_early)
     )

time: 119 us -> 123 us (1.034)
  Pallas kernels: 27.7 us -> 33 us
  other arithmetic: 14.5 us -> 16.7 us
  local copies, waits for them, and re-layouts: 6.22 us -> 4.03 us
    add x0 -> x2, other arithmetic: none -> 8.04 us  [filter_frames(): running + taps[tap_index][None, None, :] * extended[offset:offset + frame...]
    convert_element_type x2, other arithmetic: 9.11 us -> 3.1 us  [the longest x1 2.12 us: body(): early = early.astype(jnp.bfloat16).reshape(half * local, frame_len)]
    ppermute x2, waiting for transfers between devices: 15.5 us -> 9.9 us  [passed_along(): return lax.ppermute(block, axis, route)]
    all_to_all x1, waiting for transfers between devices: 8.11 us -> 12.7 us  [body(): lax.all_to_all(spec_late, BOTH, split_axis=0, concat_axis=0, tiled=True)]
    unnamed x8 -> x14, local copies, waits for them, and re-layouts: 3.4 us -> 0.04 us
    pallas_call x1, Pallas kernels: 10.5 us -> 13.3 us  [correlate(): pl.pallas_call(functools.partial(correlate_kernel, stations, blocks, own,...]
    pallas_call x2, Pallas kernels: 11.7 us -> 14.2 us  [channelise(): pl.pallas_call(functools.partial(dft_kernel, own), grid=(dests // group,)...]
    all_to_all x1, starting transfers between devices: 7.62 us -> 6.39 us  [body(): lax.all_to_all(spec_early, BOTH, split_axis=0, concat_axis=0, tiled=True)]
  transfers between devices with their start and end apart: 7 -> 7, of which waited for: 6 -> 6; matrix products, arithmetic and copies ran while one was open for 14% -> 15% of each run, Pallas kernels for 15% -> 16%
where the time goes in v4:
time: 123 us; the launch traced here: 122 us
  waiting for transfers between devices  36.4 us (30%)
  Pallas kernels  33 us (27%)
  starting transfers between devices  31.3 us (25%)
  other arithmetic  16.7 us (14%)
  local copies, waits for them, and re-layouts  4.03 us (3%)
    pallas_call x2, Pallas kernels, channelise(): pl.pallas_call(functools.partial(dft_kernel, own), grid=(dests // group,)...  14.2 us
    pallas_call x1, Pallas kernels, correlate(): pl.pallas_call(functools.partial(correlate_kernel, stations, blocks, own,...  13.3 us
    all_to_all x1, waiting for transfers between devices, body(): lax.all_to_all(spec_late, BOTH, split_axis=0, concat_axis=0, tiled=True)  12.7 us
    ppermute x2, starting transfers between devices, passed_along(): return lax.ppermute(block, axis, route)  10 us
    ppermute x2, waiting for transfers between devices, passed_along(): return lax.ppermute(block, axis, route)  9.9 us
    ppermute x3, starting transfers between devices, sum_scatter(): other = lax.ppermute(jnp.where(upper, low, high), 'station', route)  9.13 us
    all_to_all x1, waiting for transfers between devices, body(): lax.all_to_all(spec_early, BOTH, split_axis=0, concat_axis=0, tiled=True)  8.07 us
    add x2, other arithmetic, filter_frames(): running + taps[tap_index][None, None, :] * extended[offset:offset + frame...  8.04 us
  transfers between devices with their start and end apart: 7, of which 6 were waited for; matrix products, arithmetic and copies ran while one was open for 15% of the time, Pallas kernels for 16%

profile of v4, /device:TPU:1, one launch (start us, length us, event | category | flops | bytes accessed | tf_op | source)
XLA Modules:
  0.0 122.3 jit_solution(11900306857272583955)
XLA Ops:
  0.6 0.0 copy-start.2
  0.6 2.4 %slice.265 = bf16[7,32,2048]{2,1,0:T(8,128)(2,1)} slice(bf16[16,32,2048]{2,1,0:T(8,128)(2,1)} %param.3), slice={[9:16], [0:32], [0:2048]} | slice | bytes 1835008 | tf_op jit(solution)/shard_map/slice | solution.py:261
  3.0 5.0 %collective-permute-start = (bf16[7,32,2048]{2,1,0:T(8,128)(2,1)}, bf16[7,32,2048]{2,1,0:T(8,128)(2,1)}, u32[]{:S(2)}, u32[]{:S(2)}) collective-permute-start(bf16[7,32,2048]{2,1,0:T(8,128)(2,1)} %slice.265), channel_id=1, source_target_pairs={{0,1},{1,2},{2,3},{4,5},{5,6},{6,7},{8,9},{9,10},{10,11},{12,13},{... | collective-permute-start | bytes 2752520 | tf_op jit(solution)/shard_map/ppermute | solution.py:18
  8.0 1.0 fusion.42
  9.0 0.0 copy-done.2
  9.0 0.0 copy-start.5
  9.0 1.6 %fusion.47 = (bf16[8,32,2048]{2,1,0:T(8,128)(2,1)}, bf16[8,32,2048]{2,1,0:T(8,128)(2,1)}) fusion(bf16[16,32,2048]{2,1,0:T(8,128)(2,1)S(1)} %copy-done.2), kind=kLoop, calls=%fused_computation.117 | loop fusion | bytes 4194304 | tf_op jit(solution)/shard_map/slice | solution.py:34
  10.6 0.0 copy-done.5
  10.6 0.1 fusion.48
  10.7 1.1 fusion.44
  11.8 2.7 %shard_map.50.table = bf16[2048,2048]{1,0:T(8,128)(2,1)S(1)} custom-call(f32[32,2048]{1,0:T(8,128)S(1)} %get-tuple-element.51.cos_hi, f32[32,2048]{1,0:T(8,128)S(1)} %get-tuple-element.50.sin_hi, f32[32,2048]{1,0:T(8,128)S(1)} %get-tuple-element.53.cos_lo, f32[32,2048]{1,0:T(8,128)S(1)} %get-tuple-element.52.sin_lo), custom_call_target="tpu_custom_call" | custom-call | flops 16777216 | bytes 8388608 | tf_op jit(solution)/shard_map/pallas_call | solution.py:58
  14.5 0.0 copy-start
  14.5 0.0 copy-start.1
  14.5 3.7 %fusion.7 = f32[8,32,2048]{2,1,0:T(8,128)S(1)} fusion(bf16[16,32,2048]{2,1,0:T(8,128)(2,1)S(1)} %copy-done.2, f32[2048]{0:T(1024)S(1)} %bitcast.54, f32[2048]{0:T(1024)S(1)} %bitcast.49, f32[2048]{0:T(1024)S(1)} %bitcast.29, f32[2048]{0:T(1024)S(1)} %bitcast.33, f32[2048]{0:T(1024)S(1)} %bitcast.37, f32[2048]{0:T(1024)S(1)} %bitcast.41, ...), kind=kLoop, calls=%fused_computation.52 | loop fusion | flops 24641536 | bytes 13762560 | tf_op jit(solution)/shard_map/add | solution.py:34
  18.2 0.0 copy-start.3
  18.3 8.1 %collective-permute-done = bf16[7,32,2048]{2,1,0:T(8,128)(2,1)} collective-permute-done((bf16[7,32,2048]{2,1,0:T(8,128)(2,1)}, bf16[7,32,2048]{2,1,0:T(8,128)(2,1)}, u32[]{:S(2)}, u32[]{:S(2)}) %collective-permute-start) | collective-permute-done | bytes 917536 | tf_op jit(solution)/shard_map/ppermute | solution.py:18
  26.3 5.1 %collective-permute-start.1 = (bf16[8,32,2048]{2,1,0:T(8,128)(2,1)}, bf16[8,32,2048]{2,1,0:T(8,128)(2,1)}, u32[]{:S(2)}, u32[]{:S(2)}) collective-permute-start(bf16[8,32,2048]{2,1,0:T(8,128)(2,1)} %get-tuple-element.23), channel_id=1, source_target_pairs={{0,1},{1,2},{2,3},{4,5},{5,6},{6,7},{8,9},{9,10},{10,11},{12,13},{... | collective-permute-start | bytes 3145736 | tf_op jit(solution)/shard_map/ppermute | solution.py:18
  31.4 1.3 %slice_select_fusion.1 = bf16[7,32,2048]{2,1,0:T(8,128)(2,1)S(1)} fusion(bf16[7,32,2048]{2,1,0:T(8,128)(2,1)} %collective-permute-done, bf16[15,32,2048]{2,1,0:T(8,128)(2,1)} %param.4, pred[]{:T(512)S(6)} %eq.45), kind=kLoop, calls=%fused_computation.78 | loop fusion | flops 458752 | bytes 2752513 | tf_op jit(solution)/shard_map/jit(_where)/select_n | solution.py:269
  32.7 0.0 copy-done.3
  32.7 0.2 pad_maximum_fusion
  32.9 4.3 %fusion.22 = f32[8,32,2048]{2,1,0:T(8,128)} fusion(bf16[8,32,2048]{2,1,0:T(8,128)(2,1)S(1)} %copy-done.3, bf16[7,32,2048]{2,1,0:T(8,128)(2,1)S(1)} %slice_select_fusion.1, bf16[15,32,2048]{2,1,0:T(8,128)(2,1)S(1)} %pad_maximum_fusion, f32[2048]{0:T(1024)S(1)} %broadcast_multiply_fusion, f32[2048]{0:T(1024)S(1)} %bitcast.50, f32[2048]{0:T(1024)S(1)} %bitcast.30, ...), kind=kLoop, calls=%fused_computation.67 | loop fusion | flops 27262976 | bytes 6160384 | tf_op jit(solution)/shard_map/add | solution.py:34
  37.2 1.0 add_convert_fusion.1
  38.2 0.0 copy-done
  38.2 0.0 copy-done.1
  38.2 5.9 %shard_map.51 = (bf16[32,64,256]{2,1,0:T(8,128)(2,1)}, f32[8,1024]{1,0:T(8,128)S(1)}) custom-call(bf16[2048,2048]{1,0:T(8,128)(2,1)S(1)} %shard_map.50.table, bf16[256,2048]{1,0:T(8,128)(2,1)S(1)} %bitcast.27, f32[8,256]{1,0:T(8,128)S(1)} %fusion.46.pick), custom_call_target="tpu_custom_call" | custom-call | flops 2147483648 | bytes 8388608 | tf_op jit(solution)/shard_map/pallas_call | solution.py:96
  44.1 5.7 %all-to-all-start = ((bf16[32,64,256]{2,1,0:T(8,128)(2,1)}), bf16[32,64,256]{2,1,0:T(8,128)(2,1)S(1)}, u32[]{:S(2)}, u32[]{:S(2)}) async-start(bf16[32,64,256]{2,1,0:T(8,128)(2,1)} %get-tuple-element.21), calls=%async_computation | async-start | bytes 2097152 | tf_op jit(solution)/shard_map/all_to_all | solution.py:279
  49.8 0.0 copy-start.4
  49.8 1.8 %collective-permute-done.1 = bf16[8,32,2048]{2,1,0:T(8,128)(2,1)} collective-permute-done((bf16[8,32,2048]{2,1,0:T(8,128)(2,1)}, bf16[8,32,2048]{2,1,0:T(8,128)(2,1)}, u32[]{:S(2)}, u32[]{:S(2)}) %collective-permute-start.1) | collective-permute-done | bytes 1048608 | tf_op jit(solution)/shard_map/ppermute | solution.py:18
  51.6 1.3 %slice_select_fusion = bf16[8,32,2048]{2,1,0:T(8,128)(2,1)S(1)} fusion(bf16[8,32,2048]{2,1,0:T(8,128)(2,1)} %collective-permute-done.1, bf16[15,32,2048]{2,1,0:T(8,128)(2,1)} %param.4, pred[]{:T(512)S(6)} %eq.45), kind=kLoop, calls=%fused_computation.77 | loop fusion | flops 524288 | bytes 3145729 | tf_op jit(solution)/shard_map/jit(_where)/select_n | solution.py:282
  53.0 0.0 copy-done.4
  53.0 2.1 %add_convert_fusion = bf16[8,32,2048]{2,1,0:T(8,128)(2,1)} fusion(f32[8,32,2048]{2,1,0:T(8,128)S(1)} %copy-done.4, bf16[8,32,2048]{2,1,0:T(8,128)(2,1)S(1)} %slice_select_fusion, f32[2048]{0:T(1024)S(1)} %bitcast.56, f32[2048]{0:T(1024)S(1)} %bitcast.52, f32[2048]{0:T(1024)S(1)} %bitcast.32, f32[2048]{0:T(1024)S(1)} %bitcast.36, f32[2048]{0:T(1024)S(1)} %bitcast.40, ...), kind=kLoop, calls=%fused_computation.68 | loop fusion | flops 13107200 | bytes 4259840 | tf_op jit(solution)/shard_map/convert_element_type | solution.py:286
  55.1 8.3 %shard_map.52 = (bf16[32,64,256]{2,1,0:T(8,128)(2,1)}, f32[8,1024]{1,0:T(8,128)}) custom-call(bf16[2048,2048]{1,0:T(8,128)(2,1)} %copy-done, bf16[256,2048]{1,0:T(8,128)(2,1)} %bitcast.28, f32[8,256]{1,0:T(8,128)} %copy-done.1), custom_call_target="tpu_custom_call" | custom-call | flops 2147483648 | bytes 8388608 | tf_op jit(solution)/shard_map/pallas_call | solution.py:96
  63.5 0.0 copy-start.6
  63.5 12.7 %all-to-all-done.got = bf16[32,64,256]{2,1,0:T(8,128)(2,1)S(1)} async-done(((bf16[32,64,256]{2,1,0:T(8,128)(2,1)}), bf16[32,64,256]{2,1,0:T(8,128)(2,1)S(1)}, u32[]{:S(2)}, u32[]{:S(2)}) %all-to-all-start) | async-done | bytes 1048608 | tf_op jit(solution)/shard_map/all_to_all | solution.py:279
  76.2 6.4 %all-to-all-start.1 = ((bf16[32,64,256]{2,1,0:T(8,128)(2,1)}), bf16[32,64,256]{2,1,0:T(8,128)(2,1)}, u32[]{:S(2)}, u32[]{:S(2)}) async-start(bf16[32,64,256]{2,1,0:T(8,128)(2,1)} %get-tuple-element.28), calls=%async_computation.1 | async-start | bytes 2097152 | tf_op jit(solution)/shard_map/all_to_all | solution.py:293
  82.6 0.0 copy-done.6
  82.6 1.5 %collective-permute-start.2 = (f32[4,16,128]{2,1,0:T(8,128)S(1)}, f32[4,16,128]{2,1,0:T(8,128)S(1)}, u32[]{:S(2)}, u32[]{:S(2)}) collective-permute-start(f32[4,16,128]{2,1,0:T(8,128)S(1)} %slice_select_fusion.2), channel_id=1, source_target_pairs={{0,16},{4,20},{8,24},{12,28},{16,0},{20,4},{24,8},{28,12},{1,17},{... | collective-permute-start | bytes 98312 | tf_op jit(solution)/shard_map/ppermute | solution.py:244
  84.1 4.2 %collective-permute-done.2 = f32[4,16,128]{2,1,0:T(8,128)S(1)} collective-permute-done((f32[4,16,128]{2,1,0:T(8,128)S(1)}, f32[4,16,128]{2,1,0:T(8,128)S(1)}, u32[]{:S(2)}, u32[]{:S(2)}) %collective-permute-start.2) | collective-permute-done | bytes 32800 | tf_op jit(solution)/shard_map/ppermute | solution.py:244
  88.3 3.0 %collective-permute-start.3 = (f32[2,16,128]{2,1,0:T(8,128)S(1)}, f32[2,16,128]{2,1,0:T(8,128)S(1)}, u32[]{:S(2)}, u32[]{:S(2)}) collective-permute-start(f32[2,16,128]{2,1,0:T(8,128)S(1)} %slice_select_fusion.3), channel_id=1, source_target_pairs={{0,8},{4,12},{8,0},{12,4},{16,24},{20,28},{24,16},{28,20},{1,9},{5... | collective-permute-start | bytes 49160 | tf_op jit(solution)/shard_map/ppermute | solution.py:244
  91.3 1.5 %collective-permute-done.3 = f32[2,16,128]{2,1,0:T(8,128)S(1)} collective-permute-done((f32[2,16,128]{2,1,0:T(8,128)S(1)}, f32[2,16,128]{2,1,0:T(8,128)S(1)}, u32[]{:S(2)}, u32[]{:S(2)}) %collective-permute-start.3) | collective-permute-done | bytes 16416 | tf_op jit(solution)/shard_map/ppermute | solution.py:244
  92.8 4.7 %collective-permute-start.4 = (f32[1,16,128]{2,1,0:T(8,128)S(1)}, f32[1,16,128]{2,1,0:T(8,128)S(1)}, u32[]{:S(2)}, u32[]{:S(2)}) collective-permute-start(f32[1,16,128]{2,1,0:T(8,128)S(1)} %slice_select_fusion.4), channel_id=1, source_target_pairs={{0,4},{4,0},{8,12},{12,8},{16,20},{20,16},{24,28},{28,24},{1,5},{5... | collective-permute-start | bytes 24584 | tf_op jit(solution)/shard_map/ppermute | solution.py:244
  97.5 2.8 %shard_map.53.late = bf16[32,64,512]{2,1,0:T(8,128)(2,1)S(1)} custom-call(bf16[32,64,256]{2,1,0:T(8,128)(2,1)S(1)} %all-to-all-done.got), custom_call_target="tpu_custom_call" | custom-call | flops 52428800 | bytes 6291456 | tf_op jit(solution)/shard_map/pallas_call | solution.py:201
  100.3 0.0 collective-permute-done.4
  100.3 0.6 multiply_bitcast_fusion
  100.9 8.1 %all-to-all-done.1.got = bf16[32,64,256]{2,1,0:T(8,128)(2,1)} async-done(((bf16[32,64,256]{2,1,0:T(8,128)(2,1)}), bf16[32,64,256]{2,1,0:T(8,128)(2,1)}, u32[]{:S(2)}, u32[]{:S(2)}) %all-to-all-start.1) | async-done | bytes 1048608 | tf_op jit(solution)/shard_map/all_to_all | solution.py:293
  109.0 13.3 %shard_map.54 = f32[32,2,256,256]{3,2,1,0:T(8,128)} custom-call(bf16[32,64,256]{2,1,0:T(8,128)(2,1)} %all-to-all-done.1.got, bf16[32,64,512]{2,1,0:T(8,128)(2,1)S(1)} %shard_map.53.late), custom_call_target="tpu_custom_call" | custom-call | tf_op jit(solution)/shard_map/pallas_call | solution.py:220
  (10 shorter events, 0.1 us)
Async XLA Ops:
  0.6 8.4 %copy-start.2 = (bf16[16,32,2048]{2,1,0:T(8,128)(2,1)S(1)}, bf16[16,32,2048]{2,1,0:T(8,128)(2,1)}, u32[]{:S(2)}) copy-start(bf16[16,32,2048]{2,1,0:T(8,128)(2,1)} %param.3) | copy-start | bytes 6291460
  3.0 23.3 %collective-permute-start = (bf16[7,32,2048]{2,1,0:T(8,128)(2,1)}, bf16[7,32,2048]{2,1,0:T(8,128)(2,1)}, u32[]{:S(2)}, u32[]{:S(2)}) collective-permute-start(bf16[7,32,2048]{2,1,0:T(8,128)(2,1)} %slice.265), channel_id=1, source_target_pairs={{0,1},{1,2},{2,3},{4,5},{5,6},{6,7},{8,9},{9,10},{10,11},{12,13},{... | collective-permute-start | bytes 2752520 | tf_op jit(solution)/shard_map/ppermute | solution.py:18
  9.0 1.6 %copy-start.5 = (f32[16,2048]{1,0:T(8,128)S(1)}, f32[16,2048]{1,0:T(8,128)}, u32[]{:S(2)}) copy-start(f32[16,2048]{1,0:T(8,128)} %param.5) | copy-start | bytes 393220
  14.5 23.7 %copy-start = (bf16[2048,2048]{1,0:T(8,128)(2,1)}, bf16[2048,2048]{1,0:T(8,128)(2,1)S(1)}, u32[]{:S(2)}) copy-start(bf16[2048,2048]{1,0:T(8,128)(2,1)S(1)} %shard_map.50.table) | copy-start | bytes 25165828
  14.5 23.7 %copy-start.1 = (f32[8,256]{1,0:T(8,128)}, f32[8,256]{1,0:T(8,128)S(1)}, u32[]{:S(2)}) copy-start(f32[8,256]{1,0:T(8,128)S(1)} %fusion.46.pick) | copy-start | bytes 24580
  18.2 14.5 %copy-start.3 = (bf16[8,32,2048]{2,1,0:T(8,128)(2,1)S(1)}, bf16[8,32,2048]{2,1,0:T(8,128)(2,1)}, u32[]{:S(2)}) copy-start(bf16[8,32,2048]{2,1,0:T(8,128)(2,1)} %get-tuple-element.32) | copy-start | bytes 3145732
  26.3 25.3 %collective-permute-start.1 = (bf16[8,32,2048]{2,1,0:T(8,128)(2,1)}, bf16[8,32,2048]{2,1,0:T(8,128)(2,1)}, u32[]{:S(2)}, u32[]{:S(2)}) collective-permute-start(bf16[8,32,2048]{2,1,0:T(8,128)(2,1)} %get-tuple-element.23), channel_id=1, source_target_pairs={{0,1},{1,2},{2,3},{4,5},{5,6},{6,7},{8,9},{9,10},{10,11},{12,13},{... | collective-permute-start | bytes 3145736 | tf_op jit(solution)/shard_map/ppermute | solution.py:18
  44.1 32.1 %all-to-all-start = ((bf16[32,64,256]{2,1,0:T(8,128)(2,1)}), bf16[32,64,256]{2,1,0:T(8,128)(2,1)S(1)}, u32[]{:S(2)}, u32[]{:S(2)}) async-start(bf16[32,64,256]{2,1,0:T(8,128)(2,1)} %get-tuple-element.21), calls=%async_computation | async-start | bytes 2097152 | tf_op jit(solution)/shard_map/all_to_all | solution.py:279
  49.8 3.2 %copy-start.4 = (f32[8,32,2048]{2,1,0:T(8,128)S(1)}, f32[8,32,2048]{2,1,0:T(8,128)}, u32[]{:S(2)}) copy-start(f32[8,32,2048]{2,1,0:T(8,128)} %fusion.22) | copy-start | bytes 6291460
  63.5 19.2 %copy-start.6 = (f32[8,1024]{1,0:T(8,128)S(1)}, f32[8,1024]{1,0:T(8,128)}, u32[]{:S(2)}) copy-start(f32[8,1024]{1,0:T(8,128)} %get-tuple-element.30) | copy-start | bytes 98308
  76.2 32.8 %all-to-all-start.1 = ((bf16[32,64,256]{2,1,0:T(8,128)(2,1)}), bf16[32,64,256]{2,1,0:T(8,128)(2,1)}, u32[]{:S(2)}, u32[]{:S(2)}) async-start(bf16[32,64,256]{2,1,0:T(8,128)(2,1)} %get-tuple-element.28), calls=%async_computation.1 | async-start | bytes 2097152 | tf_op jit(solution)/shard_map/all_to_all | solution.py:293
  82.6 5.6 %collective-permute-start.2 = (f32[4,16,128]{2,1,0:T(8,128)S(1)}, f32[4,16,128]{2,1,0:T(8,128)S(1)}, u32[]{:S(2)}, u32[]{:S(2)}) collective-permute-start(f32[4,16,128]{2,1,0:T(8,128)S(1)} %slice_select_fusion.2), channel_id=1, source_target_pairs={{0,16},{4,20},{8,24},{12,28},{16,0},{20,4},{24,8},{28,12},{1,17},{... | collective-permute-start | bytes 98312 | tf_op jit(solution)/shard_map/ppermute | solution.py:244
  88.3 4.5 %collective-permute-start.3 = (f32[2,16,128]{2,1,0:T(8,128)S(1)}, f32[2,16,128]{2,1,0:T(8,128)S(1)}, u32[]{:S(2)}, u32[]{:S(2)}) collective-permute-start(f32[2,16,128]{2,1,0:T(8,128)S(1)} %slice_select_fusion.3), channel_id=1, source_target_pairs={{0,8},{4,12},{8,0},{12,4},{16,24},{20,28},{24,16},{28,20},{1,9},{5... | collective-permute-start | bytes 49160 | tf_op jit(solution)/shard_map/ppermute | solution.py:244
  92.8 7.5 %collective-permute-start.4 = (f32[1,16,128]{2,1,0:T(8,128)S(1)}, f32[1,16,128]{2,1,0:T(8,128)S(1)}, u32[]{:S(2)}, u32[]{:S(2)}) collective-permute-start(f32[1,16,128]{2,1,0:T(8,128)S(1)} %slice_select_fusion.4), channel_id=1, source_target_pairs={{0,4},{4,0},{8,12},{12,8},{16,20},{20,16},{24,28},{28,24},{1,5},{5... | collective-permute-start | bytes 24584 | tf_op jit(solution)/shard_map/ppermute | solution.py:244

commit v5 on v3

--- a/solution.py
+++ b/solution.py
@@ -214,7 +214,7 @@
 
 def correlate(got, late, stations, blocks, own, local, scale):
     inputs = stations * local
-    group = math.gcd(own, 4)
+    group = math.gcd(own, 8)
     return pl.pallas_call(
         functools.partial(correlate_kernel, stations, blocks, own, local, scale),
         grid=(own // group,),

time: 119 us -> 118 us (level)
  no operation moved by 1% of the time
where the time goes in v5:
time: 118 us
  waiting for transfers between devices  37.4 us (32%)
  starting transfers between devices  31.4 us (27%)
  Pallas kernels  27.3 us (23%)
  other arithmetic  14.5 us (12%)
  local copies, waits for them, and re-layouts  6.22 us (5%)
    ppermute x2, waiting for transfers between devices, passed_along(): return lax.ppermute(block, axis, route)  15.5 us
    pallas_call x2, Pallas kernels, channelise(): pl.pallas_call(functools.partial(dft_kernel, own), grid=(dests // group,)...  11.7 us
    pallas_call x1, Pallas kernels, correlate(): pl.pallas_call(functools.partial(correlate_kernel, stations, blocks, own,...  10.1 us
    ppermute x2, starting transfers between devices, passed_along(): return lax.ppermute(block, axis, route)  9.19 us
    ppermute x3, starting transfers between devices, sum_scatter(): other = lax.ppermute(jnp.where(upper, low, high), 'station', route)  9.13 us
    convert_element_type x2, other arithmetic, filter_frames(): return running.astype(jnp.bfloat16)  9.11 us
    all_to_all x1, waiting for transfers between devices, body(): lax.all_to_all(spec_late, BOTH, split_axis=0, concat_axis=0, tiled=True)  8.11 us
    all_to_all x1, waiting for transfers between devices, body(): lax.all_to_all(spec_early, BOTH, split_axis=0, concat_axis=0, tiled=True)  8.07 us
  transfers between devices with their start and end apart: 7, of which 6 were waited for; matrix products, arithmetic and copies ran while one was open for 14% of the time, Pallas kernels for 15%

profile of v5, /device:TPU:1, one launch (start us, length us, event | category | flops | bytes accessed | tf_op | source)
XLA Modules:
  0.0 117.6 jit_solution(17187071832518290833)
XLA Ops:
  0.6 1.2 %slice.200 = bf16[7,32,2048]{2,1,0:T(8,128)(2,1)S(1)} slice(bf16[16,32,2048]{2,1,0:T(8,128)(2,1)} %param.3), slice={[9:16], [0:32], [0:2048]} | slice | bytes 1835008 | tf_op jit(solution)/shard_map/slice | solution.py:259
  1.9 4.1 %collective-permute-start = (bf16[7,32,2048]{2,1,0:T(8,128)(2,1)S(1)}, bf16[7,32,2048]{2,1,0:T(8,128)(2,1)S(1)}, u32[]{:S(2)}, u32[]{:S(2)}) collective-permute-start(bf16[7,32,2048]{2,1,0:T(8,128)(2,1)S(1)} %slice.200), channel_id=1, source_target_pairs={{0,1},{1,2},{2,3},{4,5},{5,6},{6,7},{8,9},{9,10},{10,11},{12,13},{... | collective-permute-start | bytes 2752520 | tf_op jit(solution)/shard_map/ppermute | solution.py:18
  6.0 1.0 fusion.55
  7.0 1.1 fusion.57
  8.1 0.0 copy-start.3
  8.2 0.0 copy-start.2
  8.2 2.7 %shard_map.50.table = bf16[2048,2048]{1,0:T(8,128)(2,1)S(1)} custom-call(f32[32,2048]{1,0:T(8,128)S(1)} %get-tuple-element.41.cos_hi, f32[32,2048]{1,0:T(8,128)S(1)} %get-tuple-element.40.sin_hi, f32[32,2048]{1,0:T(8,128)S(1)} %get-tuple-element.43.cos_lo, f32[32,2048]{1,0:T(8,128)S(1)} %get-tuple-element.42.sin_lo), custom_call_target="tpu_custom_call" | custom-call | flops 16777216 | bytes 8388608 | tf_op jit(solution)/shard_map/pallas_call | solution.py:56
  10.8 0.0 copy-done.3
  10.9 0.0 copy-start
  10.9 0.1 fusion.61
  11.0 0.0 copy-done.2
  11.0 1.5 %fusion.60 = (bf16[8,32,2048]{2,1,0:T(8,128)(2,1)S(1)}, bf16[8,32,2048]{2,1,0:T(8,128)(2,1)}) fusion(bf16[16,32,2048]{2,1,0:T(8,128)(2,1)S(1)} %copy-done.2), kind=kLoop, calls=%fused_computation.123 | loop fusion | bytes 4194304 | tf_op jit(solution)/shard_map/slice | solution.py:34
  12.5 12.4 %collective-permute-done = bf16[7,32,2048]{2,1,0:T(8,128)(2,1)S(1)} collective-permute-done((bf16[7,32,2048]{2,1,0:T(8,128)(2,1)S(1)}, bf16[7,32,2048]{2,1,0:T(8,128)(2,1)S(1)}, u32[]{:S(2)}, u32[]{:S(2)}) %collective-permute-start) | collective-permute-done | bytes 917536 | tf_op jit(solution)/shard_map/ppermute | solution.py:18
  24.9 5.1 %collective-permute-start.1 = (bf16[8,32,2048]{2,1,0:T(8,128)(2,1)}, bf16[8,32,2048]{2,1,0:T(8,128)(2,1)}, u32[]{:S(2)}, u32[]{:S(2)}) collective-permute-start(bf16[8,32,2048]{2,1,0:T(8,128)(2,1)} %get-tuple-element.15), channel_id=1, source_target_pairs={{0,1},{1,2},{2,3},{4,5},{5,6},{6,7},{8,9},{9,10},{10,11},{12,13},{... | collective-permute-start | bytes 3145736 | tf_op jit(solution)/shard_map/ppermute | solution.py:18
  30.0 1.3 %slice_select_fusion.1 = bf16[7,32,2048]{2,1,0:T(8,128)(2,1)S(1)} fusion(bf16[7,32,2048]{2,1,0:T(8,128)(2,1)S(1)} %collective-permute-done, bf16[15,32,2048]{2,1,0:T(8,128)(2,1)} %param.4, pred[]{:T(512)S(6)} %eq.45), kind=kLoop, calls=%fused_computation.85 | loop fusion | flops 458752 | bytes 2752513 | tf_op jit(solution)/shard_map/jit(_where)/select_n | solution.py:263
  31.3 4.5 %fusion.8 = bf16[8,32,2048]{2,1,0:T(8,128)(2,1)S(1)} fusion(bf16[16,32,2048]{2,1,0:T(8,128)(2,1)S(1)} %copy-done.2, bf16[7,32,2048]{2,1,0:T(8,128)(2,1)S(1)} %slice_select_fusion.1, f32[2048]{0:T(1024)S(1)} %bitcast.57, f32[2048]{0:T(1024)S(1)} %bitcast.59, f32[2048]{0:T(1024)S(1)} %bitcast.31, f32[2048]{0:T(1024)S(1)} %bitcast.33, f32[2048]{0:T(1024)S(1)} %bitcast.35, ...), kind=kLoop, calls=%fused_computation.46 | loop fusion | flops 28835840 | bytes 13631488 | tf_op jit(solution)/shard_map/convert_element_type | solution.py:37
  35.8 0.0 copy-done
  35.9 5.9 %shard_map.51 = (bf16[32,64,256]{2,1,0:T(8,128)(2,1)}, f32[8,1024]{1,0:T(8,128)S(1)}) custom-call(bf16[2048,2048]{1,0:T(8,128)(2,1)S(1)} %shard_map.50.table, bf16[256,2048]{1,0:T(8,128)(2,1)S(1)} %bitcast.28, f32[8,256]{1,0:T(8,128)S(1)} %fusion.59.pick), custom_call_target="tpu_custom_call" | custom-call | flops 2147483648 | bytes 8388608 | tf_op jit(solution)/shard_map/pallas_call | solution.py:94
  41.7 5.4 %all-to-all-start = ((bf16[32,64,256]{2,1,0:T(8,128)(2,1)}), bf16[32,64,256]{2,1,0:T(8,128)(2,1)S(1)}, u32[]{:S(2)}, u32[]{:S(2)}) async-start(bf16[32,64,256]{2,1,0:T(8,128)(2,1)} %get-tuple-element.14), calls=%async_computation | async-start | bytes 2097152 | tf_op jit(solution)/shard_map/all_to_all | solution.py:267
  47.2 3.1 %collective-permute-done.1 = bf16[8,32,2048]{2,1,0:T(8,128)(2,1)} collective-permute-done((bf16[8,32,2048]{2,1,0:T(8,128)(2,1)}, bf16[8,32,2048]{2,1,0:T(8,128)(2,1)}, u32[]{:S(2)}, u32[]{:S(2)}) %collective-permute-start.1) | collective-permute-done | bytes 1048608 | tf_op jit(solution)/shard_map/ppermute | solution.py:18
  50.2 1.3 %slice_select_fusion = bf16[8,32,2048]{2,1,0:T(8,128)(2,1)S(1)} fusion(bf16[8,32,2048]{2,1,0:T(8,128)(2,1)} %collective-permute-done.1, bf16[15,32,2048]{2,1,0:T(8,128)(2,1)} %param.4, pred[]{:T(512)S(6)} %eq.45), kind=kLoop, calls=%fused_computation.84 | loop fusion | flops 524288 | bytes 3145729 | tf_op jit(solution)/shard_map/jit(_where)/select_n | solution.py:269
  51.6 4.6 %fusion.24 = bf16[8,32,2048]{2,1,0:T(8,128)(2,1)S(1)} fusion(bf16[8,32,2048]{2,1,0:T(8,128)(2,1)S(1)} %slice_select_fusion, bf16[8,32,2048]{2,1,0:T(8,128)(2,1)S(1)} %get-tuple-element.22, bf16[7,32,2048]{2,1,0:T(8,128)(2,1)S(1)} %slice_select_fusion.1, f32[2048]{0:T(1024)S(1)} %bitcast.58, f32[2048]{0:T(1024)S(1)} %bitcast.60, f32[2048]{0:T(1024)S(1)} %bitcast.32, ...), kind=kLoop, calls=%fused_computation.62 | loop fusion | flops 32505856 | bytes 4194304 | tf_op jit(solution)/shard_map/convert_element_type | solution.py:37
  56.2 0.0 copy-start.1
  56.2 3.4 %copy-done.1 = bf16[2048,2048]{1,0:T(8,128)(2,1)S(1)} copy-done((bf16[2048,2048]{1,0:T(8,128)(2,1)S(1)}, bf16[2048,2048]{1,0:T(8,128)(2,1)}, u32[]{:S(2)}) %copy-start.1) | copy-done | bytes 8388632
  59.5 5.9 %shard_map.52 = (bf16[32,64,256]{2,1,0:T(8,128)(2,1)}, f32[8,1024]{1,0:T(8,128)S(1)}) custom-call(bf16[2048,2048]{1,0:T(8,128)(2,1)S(1)} %copy-done.1, bf16[256,2048]{1,0:T(8,128)(2,1)S(1)} %bitcast.27, f32[8,256]{1,0:T(8,128)S(1)} %fusion.59.pick), custom_call_target="tpu_custom_call" | custom-call | flops 2147483648 | bytes 8388608 | tf_op jit(solution)/shard_map/pallas_call | solution.py:94
  65.4 8.1 %all-to-all-done.got = bf16[32,64,256]{2,1,0:T(8,128)(2,1)S(1)} async-done(((bf16[32,64,256]{2,1,0:T(8,128)(2,1)}), bf16[32,64,256]{2,1,0:T(8,128)(2,1)S(1)}, u32[]{:S(2)}, u32[]{:S(2)}) %all-to-all-start) | async-done | bytes 1048608 | tf_op jit(solution)/shard_map/all_to_all | solution.py:267
  73.5 7.6 %all-to-all-start.1 = ((bf16[32,64,256]{2,1,0:T(8,128)(2,1)}), bf16[32,64,256]{2,1,0:T(8,128)(2,1)}, u32[]{:S(2)}, u32[]{:S(2)}) async-start(bf16[32,64,256]{2,1,0:T(8,128)(2,1)} %get-tuple-element.18), calls=%async_computation.1 | async-start | bytes 2097152 | tf_op jit(solution)/shard_map/all_to_all | solution.py:276
  81.2 1.5 %collective-permute-start.2 = (f32[4,16,128]{2,1,0:T(8,128)S(1)}, f32[4,16,128]{2,1,0:T(8,128)S(1)}, u32[]{:S(2)}, u32[]{:S(2)}) collective-permute-start(f32[4,16,128]{2,1,0:T(8,128)S(1)} %slice_select_fusion.2), channel_id=1, source_target_pairs={{0,16},{4,20},{8,24},{12,28},{16,0},{20,4},{24,8},{28,12},{1,17},{... | collective-permute-start | bytes 98312 | tf_op jit(solution)/shard_map/ppermute | solution.py:242
  82.7 4.2 %collective-permute-done.2 = f32[4,16,128]{2,1,0:T(8,128)S(1)} collective-permute-done((f32[4,16,128]{2,1,0:T(8,128)S(1)}, f32[4,16,128]{2,1,0:T(8,128)S(1)}, u32[]{:S(2)}, u32[]{:S(2)}) %collective-permute-start.2) | collective-permute-done | bytes 32800 | tf_op jit(solution)/shard_map/ppermute | solution.py:242
  86.9 3.0 %collective-permute-start.3 = (f32[2,16,128]{2,1,0:T(8,128)S(1)}, f32[2,16,128]{2,1,0:T(8,128)S(1)}, u32[]{:S(2)}, u32[]{:S(2)}) collective-permute-start(f32[2,16,128]{2,1,0:T(8,128)S(1)} %slice_select_fusion.3), channel_id=1, source_target_pairs={{0,8},{4,12},{8,0},{12,4},{16,24},{20,28},{24,16},{28,20},{1,9},{5... | collective-permute-start | bytes 49160 | tf_op jit(solution)/shard_map/ppermute | solution.py:242
  89.8 1.5 %collective-permute-done.3 = f32[2,16,128]{2,1,0:T(8,128)S(1)} collective-permute-done((f32[2,16,128]{2,1,0:T(8,128)S(1)}, f32[2,16,128]{2,1,0:T(8,128)S(1)}, u32[]{:S(2)}, u32[]{:S(2)}) %collective-permute-start.3) | collective-permute-done | bytes 16416 | tf_op jit(solution)/shard_map/ppermute | solution.py:242
  91.4 4.7 %collective-permute-start.4 = (f32[1,16,128]{2,1,0:T(8,128)S(1)}, f32[1,16,128]{2,1,0:T(8,128)S(1)}, u32[]{:S(2)}, u32[]{:S(2)}) collective-permute-start(f32[1,16,128]{2,1,0:T(8,128)S(1)} %slice_select_fusion.4), channel_id=1, source_target_pairs={{0,4},{4,0},{8,12},{12,8},{16,20},{20,16},{24,28},{28,24},{1,5},{5... | collective-permute-start | bytes 24584 | tf_op jit(solution)/shard_map/ppermute | solution.py:242
  96.1 2.8 %shard_map.53.late = bf16[32,64,512]{2,1,0:T(8,128)(2,1)S(1)} custom-call(bf16[32,64,256]{2,1,0:T(8,128)(2,1)S(1)} %all-to-all-done.got), custom_call_target="tpu_custom_call" | custom-call | flops 52428800 | bytes 6291456 | tf_op jit(solution)/shard_map/pallas_call | solution.py:199
  98.9 0.0 collective-permute-done.4
  98.9 0.6 multiply_bitcast_fusion
  99.5 8.1 %all-to-all-done.1.got = bf16[32,64,256]{2,1,0:T(8,128)(2,1)} async-done(((bf16[32,64,256]{2,1,0:T(8,128)(2,1)}), bf16[32,64,256]{2,1,0:T(8,128)(2,1)}, u32[]{:S(2)}, u32[]{:S(2)}) %all-to-all-start.1) | async-done | bytes 1048608 | tf_op jit(solution)/shard_map/all_to_all | solution.py:276
  107.5 10.1 %shard_map.54 = f32[32,2,256,256]{3,2,1,0:T(8,128)} custom-call(bf16[32,64,256]{2,1,0:T(8,128)(2,1)} %all-to-all-done.1.got, bf16[32,64,512]{2,1,0:T(8,128)(2,1)S(1)} %shard_map.53.late), custom_call_target="tpu_custom_call" | custom-call | tf_op jit(solution)/shard_map/pallas_call | solution.py:218
  (9 shorter events, 0.1 us)
Async XLA Ops:
  1.9 23.0 %collective-permute-start = (bf16[7,32,2048]{2,1,0:T(8,128)(2,1)S(1)}, bf16[7,32,2048]{2,1,0:T(8,128)(2,1)S(1)}, u32[]{:S(2)}, u32[]{:S(2)}) collective-permute-start(bf16[7,32,2048]{2,1,0:T(8,128)(2,1)S(1)} %slice.200), channel_id=1, source_target_pairs={{0,1},{1,2},{2,3},{4,5},{5,6},{6,7},{8,9},{9,10},{10,11},{12,13},{... | collective-permute-start | bytes 2752520 | tf_op jit(solution)/shard_map/ppermute | solution.py:18
  8.1 2.7 %copy-start.3 = (f32[16,2048]{1,0:T(8,128)S(1)}, f32[16,2048]{1,0:T(8,128)}, u32[]{:S(2)}) copy-start(f32[16,2048]{1,0:T(8,128)} %param.5) | copy-start | bytes 393220
  8.2 2.8 %copy-start.2 = (bf16[16,32,2048]{2,1,0:T(8,128)(2,1)S(1)}, bf16[16,32,2048]{2,1,0:T(8,128)(2,1)}, u32[]{:S(2)}) copy-start(bf16[16,32,2048]{2,1,0:T(8,128)(2,1)} %param.3) | copy-start | bytes 6291460
  10.9 25.0 %copy-start = (bf16[2048,2048]{1,0:T(8,128)(2,1)}, bf16[2048,2048]{1,0:T(8,128)(2,1)S(1)}, u32[]{:S(2)}) copy-start(bf16[2048,2048]{1,0:T(8,128)(2,1)S(1)} %shard_map.50.table) | copy-start | bytes 25165828
  24.9 25.3 %collective-permute-start.1 = (bf16[8,32,2048]{2,1,0:T(8,128)(2,1)}, bf16[8,32,2048]{2,1,0:T(8,128)(2,1)}, u32[]{:S(2)}, u32[]{:S(2)}) collective-permute-start(bf16[8,32,2048]{2,1,0:T(8,128)(2,1)} %get-tuple-element.15), channel_id=1, source_target_pairs={{0,1},{1,2},{2,3},{4,5},{5,6},{6,7},{8,9},{9,10},{10,11},{12,13},{... | collective-permute-start | bytes 3145736 | tf_op jit(solution)/shard_map/ppermute | solution.py:18
  41.7 31.8 %all-to-all-start = ((bf16[32,64,256]{2,1,0:T(8,128)(2,1)}), bf16[32,64,256]{2,1,0:T(8,128)(2,1)S(1)}, u32[]{:S(2)}, u32[]{:S(2)}) async-start(bf16[32,64,256]{2,1,0:T(8,128)(2,1)} %get-tuple-element.14), calls=%async_computation | async-start | bytes 2097152 | tf_op jit(solution)/shard_map/all_to_all | solution.py:267
  56.2 3.4 %copy-start.1 = (bf16[2048,2048]{1,0:T(8,128)(2,1)S(1)}, bf16[2048,2048]{1,0:T(8,128)(2,1)}, u32[]{:S(2)}) copy-start(bf16[2048,2048]{1,0:T(8,128)(2,1)} %copy-done) | copy-start | bytes 25165828
  73.5 34.0 %all-to-all-start.1 = ((bf16[32,64,256]{2,1,0:T(8,128)(2,1)}), bf16[32,64,256]{2,1,0:T(8,128)(2,1)}, u32[]{:S(2)}, u32[]{:S(2)}) async-start(bf16[32,64,256]{2,1,0:T(8,128)(2,1)} %get-tuple-element.18), calls=%async_computation.1 | async-start | bytes 2097152 | tf_op jit(solution)/shard_map/all_to_all | solution.py:276
  81.2 5.6 %collective-permute-start.2 = (f32[4,16,128]{2,1,0:T(8,128)S(1)}, f32[4,16,128]{2,1,0:T(8,128)S(1)}, u32[]{:S(2)}, u32[]{:S(2)}) collective-permute-start(f32[4,16,128]{2,1,0:T(8,128)S(1)} %slice_select_fusion.2), channel_id=1, source_target_pairs={{0,16},{4,20},{8,24},{12,28},{16,0},{20,4},{24,8},{28,12},{1,17},{... | collective-permute-start | bytes 98312 | tf_op jit(solution)/shard_map/ppermute | solution.py:242
  86.9 4.5 %collective-permute-start.3 = (f32[2,16,128]{2,1,0:T(8,128)S(1)}, f32[2,16,128]{2,1,0:T(8,128)S(1)}, u32[]{:S(2)}, u32[]{:S(2)}) collective-permute-start(f32[2,16,128]{2,1,0:T(8,128)S(1)} %slice_select_fusion.3), channel_id=1, source_target_pairs={{0,8},{4,12},{8,0},{12,4},{16,24},{20,28},{24,16},{28,20},{1,9},{5... | collective-permute-start | bytes 49160 | tf_op jit(solution)/shard_map/ppermute | solution.py:242
  91.4 7.5 %collective-permute-start.4 = (f32[1,16,128]{2,1,0:T(8,128)S(1)}, f32[1,16,128]{2,1,0:T(8,128)S(1)}, u32[]{:S(2)}, u32[]{:S(2)}) collective-permute-start(f32[1,16,128]{2,1,0:T(8,128)S(1)} %slice_select_fusion.4), channel_id=1, source_target_pairs={{0,4},{4,0},{8,12},{12,8},{16,20},{20,16},{24,28},{28,24},{1,5},{5... | collective-permute-start | bytes 24584 | tf_op jit(solution)/shard_map/ppermute | solution.py:242

commit v6 on v4

--- a/solution.py
+++ b/solution.py
@@ -9,7 +9,7 @@
 from jax.sharding import PartitionSpec as P
 
 BOTH = ("station", "tm")
-VMEM_LIMIT = 14 * 1024 * 1024
+VMEM_LIMIT = 24 * 1024 * 1024
 
 
 def passed_along(block, axis, distance):
@@ -52,7 +52,9 @@
         )
 
 
-def dft_table(angles, own, dests, group, frame_len):
+def dft_table(own, dests, group, frame_len):
+    cos_hi, sin_hi = angle_tables(dests, own, frame_len)
+    cos_lo, sin_lo = angle_tables(own, 1, frame_len)
     high = pl.BlockSpec((group, frame_len), lambda i: (i, 0))
     low = pl.BlockSpec((own, frame_len), lambda i: (0, 0))
     return pl.pallas_call(
@@ -67,7 +69,7 @@
             bytes_accessed=dests * own * frame_len * 4,
             transcendentals=0,
         ),
-    )(*angles)
+    )(cos_hi, sin_hi, cos_lo, sin_lo)
 
 
 def dft_kernel(own, table, weighted, pick, spec, power):
@@ -216,7 +218,7 @@
 
 def correlate(got, late, stations, blocks, own, local, scale):
     inputs = stations * local
-    group = math.gcd(own, 2)
+    group = math.gcd(own, 8)
     return pl.pallas_call(
         functools.partial(correlate_kernel, stations, blocks, own, local, scale),
         grid=(own // group,),
@@ -259,8 +261,7 @@
     tail = samples[frames_dev - span :]
 
     near = passed_along(tail[half:], "tm", 1)
-    angles = angle_tables(dests, own, frame_len) + angle_tables(own, 1, frame_len)
-    table = dft_table(angles, own, dests, group, frame_len)
+    table = dft_table(own, dests, group, frame_len)
     own_late = filter_frames(padded(samples, span - half, 0), taps, half)
     near, far_tail, table, own_late = lax.optimization_barrier(
         (near, tail[:half], table, own_late)
@@ -269,23 +270,17 @@
     near = jnp.where(first, history[half:], near)
     late = own_late + filter_frames(padded(near, 0, half), taps, half, half + 1)
     late = late.astype(jnp.bfloat16).reshape(half * local, frame_len)
-    own_early = filter_frames(
-        padded(jnp.concatenate([near, samples[:half]], axis=0), half, 0), taps, half
-    )
-    late, own_early = lax.optimization_barrier((late, own_early))
     spec_late, power_late = channelise(
         table, late, own, half, dests, group, VMEM_LIMIT
     )
     got_late = lax.all_to_all(spec_late, BOTH, split_axis=0, concat_axis=0, tiled=True)
 
-    far, spec_late, power_late = lax.optimization_barrier((far, spec_late, power_late))
+    far, near, late = lax.optimization_barrier((far, near, late))
     far = jnp.where(first, history[:half], far)
-    early = own_early + filter_frames(
-        padded(far, 0, span - half), taps, half, span - half + 1
-    )
+    early = filter_frames(jnp.concatenate([far, near, samples[:half]], axis=0), taps, half)
     early = early.astype(jnp.bfloat16).reshape(half * local, frame_len)
     spec_early, power_early = channelise(
-        table, early, own, half, dests, group, 4 * VMEM_LIMIT
+        table, early, own, half, dests, group, 56 * 1024 * 1024
     )
     got_late, spec_early, power_early = lax.optimization_barrier(
         (got_late, spec_early, power_early)

time: 123 us -> 120 us (0.976)
  starting transfers between devices: 31.3 us -> 35.7 us
  Pallas kernels: 33 us -> 29.7 us
  waiting for transfers between devices: 36.4 us -> 33.2 us
    all_to_all x1, waiting for transfers between devices: 12.7 us -> 5.05 us  [body(): lax.all_to_all(spec_late, BOTH, split_axis=0, concat_axis=0, tiled=True)]
    ppermute x2, waiting for transfers between devices: 9.9 us -> 14.3 us  [passed_along(): return lax.ppermute(block, axis, route)]
    all_to_all x1, starting transfers between devices: 6.39 us -> 10.8 us  [body(): lax.all_to_all(spec_early, BOTH, split_axis=0, concat_axis=0, tiled=True)]
    add x2 -> x1, other arithmetic: 8.04 us -> 3.75 us  [filter_frames(): running + taps[tap_index][None, None, :] * extended[offset:offset + frame...]
    pallas_call x1, Pallas kernels: 13.3 us -> 10.1 us  [correlate(): pl.pallas_call(functools.partial(correlate_kernel, stations, blocks, own,...]
    convert_element_type x1, other arithmetic: 2.12 us -> 5.34 us  [body(): early = early.astype(jnp.bfloat16).reshape(half * local, frame_len)]
  transfers between devices with their start and end apart: 7 -> 7, of which waited for: 6 -> 6; matrix products, arithmetic and copies ran while one was open for 15% -> 14% of each run, Pallas kernels for 16% -> 17%
where the time goes in v6:
time: 120 us; the launch traced here: 119 us
  starting transfers between devices  35.7 us (30%)
  waiting for transfers between devices  33.2 us (28%)
  Pallas kernels  29.7 us (25%)
  other arithmetic  15.5 us (13%)
  local copies, waits for them, and re-layouts  4.06 us (3%)
    ppermute x2, waiting for transfers between devices, passed_along(): return lax.ppermute(block, axis, route)  14.3 us
    pallas_call x2, Pallas kernels, channelise(): pl.pallas_call(functools.partial(dft_kernel, own), grid=(dests // group,)...  14.2 us
    all_to_all x1, starting transfers between devices, body(): lax.all_to_all(spec_early, BOTH, split_axis=0, concat_axis=0, tiled=True)  10.8 us
    pallas_call x1, Pallas kernels, correlate(): pl.pallas_call(functools.partial(correlate_kernel, stations, blocks, own,...  10.1 us
    ppermute x2, starting transfers between devices, passed_along(): return lax.ppermute(block, axis, route)  10.1 us
    ppermute x3, starting transfers between devices, sum_scatter(): other = lax.ppermute(jnp.where(upper, low, high), 'station', route)  9.13 us
    all_to_all x1, waiting for transfers between devices, body(): lax.all_to_all(spec_early, BOTH, split_axis=0, concat_axis=0, tiled=True)  8.07 us
    ppermute x3, waiting for transfers between devices, sum_scatter(): other = lax.ppermute(jnp.where(upper, low, high), 'station', route)  5.7 us
  transfers between devices with their start and end apart: 7, of which 6 were waited for; matrix products, arithmetic and copies ran while one was open for 14% of the time, Pallas kernels for 17%

profile of v6, /device:TPU:1, one launch (start us, length us, event | category | flops | bytes accessed | tf_op | source)
XLA Modules:
  0.0 119.1 jit_solution(10627088686351574934)
XLA Ops:
  0.6 0.0 copy-start.2
  0.6 2.4 %slice.237 = bf16[7,32,2048]{2,1,0:T(8,128)(2,1)} slice(bf16[16,32,2048]{2,1,0:T(8,128)(2,1)} %param.3), slice={[9:16], [0:32], [0:2048]} | slice | bytes 1835008 | tf_op jit(solution)/shard_map/slice | solution.py:263
  3.0 5.0 %collective-permute-start = (bf16[7,32,2048]{2,1,0:T(8,128)(2,1)}, bf16[7,32,2048]{2,1,0:T(8,128)(2,1)}, u32[]{:S(2)}, u32[]{:S(2)}) collective-permute-start(bf16[7,32,2048]{2,1,0:T(8,128)(2,1)} %slice.237), channel_id=1, source_target_pairs={{0,1},{1,2},{2,3},{4,5},{5,6},{6,7},{8,9},{9,10},{10,11},{12,13},{... | collective-permute-start | bytes 2752520 | tf_op jit(solution)/shard_map/ppermute | solution.py:18
  8.0 1.0 fusion.48
  9.0 0.0 copy-done.2
  9.0 0.0 copy-start.4
  9.0 1.6 %fusion.53 = (bf16[8,32,2048]{2,1,0:T(8,128)(2,1)}, bf16[8,32,2048]{2,1,0:T(8,128)(2,1)}) fusion(bf16[16,32,2048]{2,1,0:T(8,128)(2,1)S(1)} %copy-done.2), kind=kLoop, calls=%fused_computation.118 | loop fusion | bytes 4194304 | tf_op jit(solution)/shard_map/slice | solution.py:34
  10.6 0.0 copy-done.4
  10.6 0.1 fusion.54
  10.7 1.1 fusion.50
  11.8 2.7 %shard_map.50.table = bf16[2048,2048]{1,0:T(8,128)(2,1)S(1)} custom-call(f32[32,2048]{1,0:T(8,128)S(1)} %get-tuple-element.47.cos_hi, f32[32,2048]{1,0:T(8,128)S(1)} %get-tuple-element.46.sin_hi, f32[32,2048]{1,0:T(8,128)S(1)} %get-tuple-element.49.cos_lo, f32[32,2048]{1,0:T(8,128)S(1)} %get-tuple-element.48.sin_lo), custom_call_target="tpu_custom_call" | custom-call | flops 16777216 | bytes 8388608 | tf_op jit(solution)/shard_map/pallas_call | solution.py:60
  14.5 0.0 copy-start
  14.5 0.0 copy-start.1
  14.5 3.8 %fusion.7 = f32[8,32,2048]{2,1,0:T(8,128)S(1)} fusion(bf16[16,32,2048]{2,1,0:T(8,128)(2,1)S(1)} %copy-done.2, f32[2048]{0:T(1024)S(1)} %bitcast.44, f32[2048]{0:T(1024)S(1)} %bitcast.47, f32[2048]{0:T(1024)S(1)} %bitcast.29, f32[2048]{0:T(1024)S(1)} %bitcast.32, f32[2048]{0:T(1024)S(1)} %bitcast.35, f32[2048]{0:T(1024)S(1)} %bitcast.38, ...), kind=kLoop, calls=%fused_computation.47 | loop fusion | flops 24641536 | bytes 13762560 | tf_op jit(solution)/shard_map/add | solution.py:34
  18.3 8.1 %collective-permute-done = bf16[7,32,2048]{2,1,0:T(8,128)(2,1)} collective-permute-done((bf16[7,32,2048]{2,1,0:T(8,128)(2,1)}, bf16[7,32,2048]{2,1,0:T(8,128)(2,1)}, u32[]{:S(2)}, u32[]{:S(2)}) %collective-permute-start) | collective-permute-done | bytes 917536 | tf_op jit(solution)/shard_map/ppermute | solution.py:18
  26.4 5.1 %collective-permute-start.1 = (bf16[8,32,2048]{2,1,0:T(8,128)(2,1)}, bf16[8,32,2048]{2,1,0:T(8,128)(2,1)}, u32[]{:S(2)}, u32[]{:S(2)}) collective-permute-start(bf16[8,32,2048]{2,1,0:T(8,128)(2,1)} %get-tuple-element.19), channel_id=1, source_target_pairs={{0,1},{1,2},{2,3},{4,5},{5,6},{6,7},{8,9},{9,10},{10,11},{12,13},{... | collective-permute-start | bytes 3145736 | tf_op jit(solution)/shard_map/ppermute | solution.py:18
  31.5 1.3 %slice_select_fusion.1 = bf16[7,32,2048]{2,1,0:T(8,128)(2,1)S(1)} fusion(bf16[7,32,2048]{2,1,0:T(8,128)(2,1)} %collective-permute-done, bf16[15,32,2048]{2,1,0:T(8,128)(2,1)} %param.4, pred[]{:T(512)S(6)} %eq.45), kind=kLoop, calls=%fused_computation.80 | loop fusion | flops 458752 | bytes 2752513 | tf_op jit(solution)/shard_map/jit(_where)/select_n | solution.py:270
  32.7 1.0 add_convert_fusion
  33.8 0.0 copy-done
  33.8 0.0 copy-done.1
  33.8 5.9 %shard_map.51 = (bf16[32,64,256]{2,1,0:T(8,128)(2,1)}, f32[8,1024]{1,0:T(8,128)S(1)}) custom-call(bf16[2048,2048]{1,0:T(8,128)(2,1)S(1)} %shard_map.50.table, bf16[256,2048]{1,0:T(8,128)(2,1)S(1)} %bitcast.27, f32[8,256]{1,0:T(8,128)S(1)} %fusion.52.pick), custom_call_target="tpu_custom_call" | custom-call | flops 2147483648 | bytes 8388608 | tf_op jit(solution)/shard_map/pallas_call | solution.py:98
  39.7 5.7 %all-to-all-start = ((bf16[32,64,256]{2,1,0:T(8,128)(2,1)}), bf16[32,64,256]{2,1,0:T(8,128)(2,1)S(1)}, u32[]{:S(2)}, u32[]{:S(2)}) async-start(bf16[32,64,256]{2,1,0:T(8,128)(2,1)} %get-tuple-element.18), calls=%async_computation | async-start | bytes 2097152 | tf_op jit(solution)/shard_map/all_to_all | solution.py:276
  45.4 0.0 copy-start.3
  45.4 6.3 %collective-permute-done.1 = bf16[8,32,2048]{2,1,0:T(8,128)(2,1)} collective-permute-done((bf16[8,32,2048]{2,1,0:T(8,128)(2,1)}, bf16[8,32,2048]{2,1,0:T(8,128)(2,1)}, u32[]{:S(2)}, u32[]{:S(2)}) %collective-permute-start.1) | collective-permute-done | bytes 1048608 | tf_op jit(solution)/shard_map/ppermute | solution.py:18
  51.7 1.3 %slice_select_fusion = bf16[8,32,2048]{2,1,0:T(8,128)(2,1)S(1)} fusion(bf16[8,32,2048]{2,1,0:T(8,128)(2,1)} %collective-permute-done.1, bf16[15,32,2048]{2,1,0:T(8,128)(2,1)} %param.4, pred[]{:T(512)S(6)} %eq.45), kind=kLoop, calls=%fused_computation.79 | loop fusion | flops 524288 | bytes 3145729 | tf_op jit(solution)/shard_map/jit(_where)/select_n | solution.py:279
  53.0 0.0 copy-done.3
  53.0 5.3 %fusion.23 = bf16[8,32,2048]{2,1,0:T(8,128)(2,1)} fusion(bf16[8,32,2048]{2,1,0:T(8,128)(2,1)S(1)} %slice_select_fusion, bf16[8,32,2048]{2,1,0:T(8,128)(2,1)S(1)} %copy-done.3, bf16[7,32,2048]{2,1,0:T(8,128)(2,1)S(1)} %slice_select_fusion.1, f32[2048]{0:T(1024)S(1)} %bitcast.46, f32[2048]{0:T(1024)S(1)} %bitcast.49, f32[2048]{0:T(1024)S(1)} %bitcast.31, ...), kind=kLoop, calls=%fused_computation.64 | loop fusion | flops 32505856 | bytes 4194304 | tf_op jit(solution)/shard_map/convert_element_type | solution.py:281
  58.4 8.3 %shard_map.52 = (bf16[32,64,256]{2,1,0:T(8,128)(2,1)}, f32[8,1024]{1,0:T(8,128)}) custom-call(bf16[2048,2048]{1,0:T(8,128)(2,1)} %copy-done, bf16[256,2048]{1,0:T(8,128)(2,1)} %bitcast.28, f32[8,256]{1,0:T(8,128)} %copy-done.1), custom_call_target="tpu_custom_call" | custom-call | flops 2147483648 | bytes 8388608 | tf_op jit(solution)/shard_map/pallas_call | solution.py:98
  66.7 0.0 copy-start.5
  66.7 5.0 %all-to-all-done.got = bf16[32,64,256]{2,1,0:T(8,128)(2,1)S(1)} async-done(((bf16[32,64,256]{2,1,0:T(8,128)(2,1)}), bf16[32,64,256]{2,1,0:T(8,128)(2,1)S(1)}, u32[]{:S(2)}, u32[]{:S(2)}) %all-to-all-start) | async-done | bytes 1048608 | tf_op jit(solution)/shard_map/all_to_all | solution.py:276
  71.8 10.8 %all-to-all-start.1 = ((bf16[32,64,256]{2,1,0:T(8,128)(2,1)}), bf16[32,64,256]{2,1,0:T(8,128)(2,1)}, u32[]{:S(2)}, u32[]{:S(2)}) async-start(bf16[32,64,256]{2,1,0:T(8,128)(2,1)} %get-tuple-element.24), calls=%async_computation.1 | async-start | bytes 2097152 | tf_op jit(solution)/shard_map/all_to_all | solution.py:288
  82.6 0.0 copy-done.5
  82.7 1.5 %collective-permute-start.2 = (f32[4,16,128]{2,1,0:T(8,128)S(1)}, f32[4,16,128]{2,1,0:T(8,128)S(1)}, u32[]{:S(2)}, u32[]{:S(2)}) collective-permute-start(f32[4,16,128]{2,1,0:T(8,128)S(1)} %slice_select_fusion.2), channel_id=1, source_target_pairs={{0,16},{4,20},{8,24},{12,28},{16,0},{20,4},{24,8},{28,12},{1,17},{... | collective-permute-start | bytes 98312 | tf_op jit(solution)/shard_map/ppermute | solution.py:246
  84.1 4.2 %collective-permute-done.2 = f32[4,16,128]{2,1,0:T(8,128)S(1)} collective-permute-done((f32[4,16,128]{2,1,0:T(8,128)S(1)}, f32[4,16,128]{2,1,0:T(8,128)S(1)}, u32[]{:S(2)}, u32[]{:S(2)}) %collective-permute-start.2) | collective-permute-done | bytes 32800 | tf_op jit(solution)/shard_map/ppermute | solution.py:246
  88.3 3.0 %collective-permute-start.3 = (f32[2,16,128]{2,1,0:T(8,128)S(1)}, f32[2,16,128]{2,1,0:T(8,128)S(1)}, u32[]{:S(2)}, u32[]{:S(2)}) collective-permute-start(f32[2,16,128]{2,1,0:T(8,128)S(1)} %slice_select_fusion.3), channel_id=1, source_target_pairs={{0,8},{4,12},{8,0},{12,4},{16,24},{20,28},{24,16},{28,20},{1,9},{5... | collective-permute-start | bytes 49160 | tf_op jit(solution)/shard_map/ppermute | solution.py:246
  91.3 1.5 %collective-permute-done.3 = f32[2,16,128]{2,1,0:T(8,128)S(1)} collective-permute-done((f32[2,16,128]{2,1,0:T(8,128)S(1)}, f32[2,16,128]{2,1,0:T(8,128)S(1)}, u32[]{:S(2)}, u32[]{:S(2)}) %collective-permute-start.3) | collective-permute-done | bytes 16416 | tf_op jit(solution)/shard_map/ppermute | solution.py:246
  92.8 4.7 %collective-permute-start.4 = (f32[1,16,128]{2,1,0:T(8,128)S(1)}, f32[1,16,128]{2,1,0:T(8,128)S(1)}, u32[]{:S(2)}, u32[]{:S(2)}) collective-permute-start(f32[1,16,128]{2,1,0:T(8,128)S(1)} %slice_select_fusion.4), channel_id=1, source_target_pairs={{0,4},{4,0},{8,12},{12,8},{16,20},{20,16},{24,28},{28,24},{1,5},{5... | collective-permute-start | bytes 24584 | tf_op jit(solution)/shard_map/ppermute | solution.py:246
  97.5 2.8 %shard_map.53.late = bf16[32,64,512]{2,1,0:T(8,128)(2,1)S(1)} custom-call(bf16[32,64,256]{2,1,0:T(8,128)(2,1)S(1)} %all-to-all-done.got), custom_call_target="tpu_custom_call" | custom-call | flops 52428800 | bytes 6291456 | tf_op jit(solution)/shard_map/pallas_call | solution.py:203
  100.3 0.0 collective-permute-done.4
  100.3 0.6 multiply_bitcast_fusion
  100.9 8.1 %all-to-all-done.1.got = bf16[32,64,256]{2,1,0:T(8,128)(2,1)} async-done(((bf16[32,64,256]{2,1,0:T(8,128)(2,1)}), bf16[32,64,256]{2,1,0:T(8,128)(2,1)}, u32[]{:S(2)}, u32[]{:S(2)}) %all-to-all-start.1) | async-done | bytes 1048608 | tf_op jit(solution)/shard_map/all_to_all | solution.py:288
  109.0 10.1 %shard_map.54 = f32[32,2,256,256]{3,2,1,0:T(8,128)} custom-call(bf16[32,64,256]{2,1,0:T(8,128)(2,1)} %all-to-all-done.1.got, bf16[32,64,512]{2,1,0:T(8,128)(2,1)S(1)} %shard_map.53.late), custom_call_target="tpu_custom_call" | custom-call | tf_op jit(solution)/shard_map/pallas_call | solution.py:222
  (9 shorter events, 0.1 us)
Async XLA Ops:
  0.6 8.4 %copy-start.2 = (bf16[16,32,2048]{2,1,0:T(8,128)(2,1)S(1)}, bf16[16,32,2048]{2,1,0:T(8,128)(2,1)}, u32[]{:S(2)}) copy-start(bf16[16,32,2048]{2,1,0:T(8,128)(2,1)} %param.3) | copy-start | bytes 6291460
  3.0 23.3 %collective-permute-start = (bf16[7,32,2048]{2,1,0:T(8,128)(2,1)}, bf16[7,32,2048]{2,1,0:T(8,128)(2,1)}, u32[]{:S(2)}, u32[]{:S(2)}) collective-permute-start(bf16[7,32,2048]{2,1,0:T(8,128)(2,1)} %slice.237), channel_id=1, source_target_pairs={{0,1},{1,2},{2,3},{4,5},{5,6},{6,7},{8,9},{9,10},{10,11},{12,13},{... | collective-permute-start | bytes 2752520 | tf_op jit(solution)/shard_map/ppermute | solution.py:18
  9.0 1.6 %copy-start.4 = (f32[16,2048]{1,0:T(8,128)S(1)}, f32[16,2048]{1,0:T(8,128)}, u32[]{:S(2)}) copy-start(f32[16,2048]{1,0:T(8,128)} %param.5) | copy-start | bytes 393220
  14.5 19.3 %copy-start = (bf16[2048,2048]{1,0:T(8,128)(2,1)}, bf16[2048,2048]{1,0:T(8,128)(2,1)S(1)}, u32[]{:S(2)}) copy-start(bf16[2048,2048]{1,0:T(8,128)(2,1)S(1)} %shard_map.50.table) | copy-start | bytes 25165828
  14.5 19.3 %copy-start.1 = (f32[8,256]{1,0:T(8,128)}, f32[8,256]{1,0:T(8,128)S(1)}, u32[]{:S(2)}) copy-start(f32[8,256]{1,0:T(8,128)S(1)} %fusion.52.pick) | copy-start | bytes 24580
  26.4 25.3 %collective-permute-start.1 = (bf16[8,32,2048]{2,1,0:T(8,128)(2,1)}, bf16[8,32,2048]{2,1,0:T(8,128)(2,1)}, u32[]{:S(2)}, u32[]{:S(2)}) collective-permute-start(bf16[8,32,2048]{2,1,0:T(8,128)(2,1)} %get-tuple-element.19), channel_id=1, source_target_pairs={{0,1},{1,2},{2,3},{4,5},{5,6},{6,7},{8,9},{9,10},{10,11},{12,13},{... | collective-permute-start | bytes 3145736 | tf_op jit(solution)/shard_map/ppermute | solution.py:18
  39.7 32.1 %all-to-all-start = ((bf16[32,64,256]{2,1,0:T(8,128)(2,1)}), bf16[32,64,256]{2,1,0:T(8,128)(2,1)S(1)}, u32[]{:S(2)}, u32[]{:S(2)}) async-start(bf16[32,64,256]{2,1,0:T(8,128)(2,1)} %get-tuple-element.18), calls=%async_computation | async-start | bytes 2097152 | tf_op jit(solution)/shard_map/all_to_all | solution.py:276
  45.4 7.6 %copy-start.3 = (bf16[8,32,2048]{2,1,0:T(8,128)(2,1)S(1)}, bf16[8,32,2048]{2,1,0:T(8,128)(2,1)}, u32[]{:S(2)}) copy-start(bf16[8,32,2048]{2,1,0:T(8,128)(2,1)} %get-tuple-element.28) | copy-start | bytes 3145732
  66.7 15.9 %copy-start.5 = (f32[8,1024]{1,0:T(8,128)S(1)}, f32[8,1024]{1,0:T(8,128)}, u32[]{:S(2)}) copy-start(f32[8,1024]{1,0:T(8,128)} %get-tuple-element.26) | copy-start | bytes 98308
  71.8 37.2 %all-to-all-start.1 = ((bf16[32,64,256]{2,1,0:T(8,128)(2,1)}), bf16[32,64,256]{2,1,0:T(8,128)(2,1)}, u32[]{:S(2)}, u32[]{:S(2)}) async-start(bf16[32,64,256]{2,1,0:T(8,128)(2,1)} %get-tuple-element.24), calls=%async_computation.1 | async-start | bytes 2097152 | tf_op jit(solution)/shard_map/all_to_all | solution.py:288
  82.7 5.6 %collective-permute-start.2 = (f32[4,16,128]{2,1,0:T(8,128)S(1)}, f32[4,16,128]{2,1,0:T(8,128)S(1)}, u32[]{:S(2)}, u32[]{:S(2)}) collective-permute-start(f32[4,16,128]{2,1,0:T(8,128)S(1)} %slice_select_fusion.2), channel_id=1, source_target_pairs={{0,16},{4,20},{8,24},{12,28},{16,0},{20,4},{24,8},{28,12},{1,17},{... | collective-permute-start | bytes 98312 | tf_op jit(solution)/shard_map/ppermute | solution.py:246
  88.3 4.5 %collective-permute-start.3 = (f32[2,16,128]{2,1,0:T(8,128)S(1)}, f32[2,16,128]{2,1,0:T(8,128)S(1)}, u32[]{:S(2)}, u32[]{:S(2)}) collective-permute-start(f32[2,16,128]{2,1,0:T(8,128)S(1)} %slice_select_fusion.3), channel_id=1, source_target_pairs={{0,8},{4,12},{8,0},{12,4},{16,24},{20,28},{24,16},{28,20},{1,9},{5... | collective-permute-start | bytes 49160 | tf_op jit(solution)/shard_map/ppermute | solution.py:246
  92.8 7.5 %collective-permute-start.4 = (f32[1,16,128]{2,1,0:T(8,128)S(1)}, f32[1,16,128]{2,1,0:T(8,128)S(1)}, u32[]{:S(2)}, u32[]{:S(2)}) collective-permute-start(f32[1,16,128]{2,1,0:T(8,128)S(1)} %slice_select_fusion.4), channel_id=1, source_target_pairs={{0,4},{4,0},{8,12},{12,8},{16,20},{20,16},{24,28},{28,24},{1,5},{5... | collective-permute-start | bytes 24584 | tf_op jit(solution)/shard_map/ppermute | solution.py:246
